TPU v7x, 128 devices: a whole 4x4x4 slice. The times are simulated.
128 devices in a mesh: dp: 8 (over z, core), tensor: 16 (over x, y).
Axes of the slice: x: 4, y: 4, z: 4, core: 2. Of those that a mesh axis runs over, the one named last changes fastest.
Arguments:
- queries: bfloat16 [4096, 36864], P('dp', 'tensor'), may hold values from -6.8560344 to 6.8560344
- cache: bfloat16 [8, 3072, 576], P('dp', 'tensor'), may hold values from -4 to 4
- offsets: int32 [8], P('dp'), may hold values from 0 to 2560, as said below
- value_up: bfloat16 [64, 512, 128], P('tensor'), may hold values from -0.25 to 0.25
- out_proj: bfloat16 [8192, 3584], P('tensor', 'dp'), may hold values from -0.0625 to 0.0625
- resid: bfloat16 [4096, 3584], P(('dp', 'tensor')), may hold values from -3 to 3
- norm_gain: float32 [3584], replicated, may hold values from 0.25 to 1.75
- routes: int32 [4096, 8], P(('dp', 'tensor')), may hold values from 0 to 127, as said below
- route_weights: float32 [4096, 8], P(('dp', 'tensor')), may hold values from 0.1 to 0.6
- expert_in: bfloat16 [128, 3584, 2048], P(('dp', 'tensor')), may hold values from -0.09375 to 0.09375
- expert_down: bfloat16 [128, 1024, 3584], P(('dp', 'tensor')), may hold values from -0.1875 to 0.1875
Outputs:
- mixed: bfloat16 [4096, 3584], P(('dp', 'tensor'))
Inputs may be any that keep to these rules, and one draw needn't show every extreme that they name: `routes`: each row names 8 different experts. Among the 32 rows of one device (aligned blocks of rows) a quarter of the experts is named 4 times, a quarter 3 times, a quarter once and a quarter never; in every draw one expert is named 4 times in every block. `offsets`: some sequence's offset is 2560; the new tokens' own latents are in the cache at their positions.
All inputs are finite; a program needn't handle non-finite values.
Results may differ from a plain program's by a relative error of at most 0.024.
Values may be sent and summed in bfloat16 or wider, within the bound.
A program may use at most 192 MiB of HBM per device.

v0:
```python
import jax
import jax.numpy as jnp
from jax import lax
from jax.sharding import PartitionSpec as P


def shards(
    queries,
    cache,
    offsets,
    value_up,
    out_proj,
    resid,
    norm_gain,
    routes,
    route_weights,
    expert_in,
    expert_down,
):
    heads_dev = value_up.shape[0]
    latent_width = value_up.shape[1]
    key_width = cache.shape[2]
    tok_grp = queries.shape[0]
    score_scale = (value_up.shape[2] + key_width - latent_width) ** (-0.5)
    query_heads = queries.reshape(tok_grp, heads_dev, key_width)
    start_pos = offsets[0]
    query_pos = start_pos + jnp.arange(tok_grp, dtype=jnp.int32)
    running = jnp.full((heads_dev, tok_grp), -1e30, jnp.float32)
    key_rows = lax.all_gather(cache, "tensor", axis=1, tiled=True)[0]
    key_count = key_rows.shape[0]
    scores = (
        jnp.einsum("thc,kc->htk", query_heads, key_rows, preferred_element_type=jnp.float32)
        * score_scale
    )
    key_pos = jnp.arange(key_count, dtype=jnp.int32)
    visible = key_pos[None, :] <= query_pos[:, None]
    scores = jnp.where(visible[None], scores, jnp.float32(-1e30))
    highest = jnp.maximum(running, jnp.max(scores, axis=2))
    weights = jnp.where(visible[None], jnp.exp(scores - highest[..., None]), jnp.float32(0.0))
    totals = jnp.sum(weights, axis=2)
    weighted = jnp.einsum(
        "htk,kc->htc",
        weights.astype(jnp.bfloat16),
        key_rows[:, :latent_width],
        preferred_element_type=jnp.float32,
    )
    running, totals, weighted = (highest, totals, weighted)
    context = (weighted / totals[..., None]).astype(jnp.bfloat16)
    head_out = jnp.einsum("htc,hcv->thv", context, value_up, preferred_element_type=jnp.float32)
    head_out = head_out.astype(jnp.bfloat16).reshape(tok_grp, -1)
    partial_value = jnp.dot(
        head_out,
        lax.all_gather(out_proj, "dp", axis=1, tiled=True),
        preferred_element_type=jnp.float32,
    )
    tok_dev = resid.shape[0]
    summed_all = lax.psum(partial_value.astype(jnp.bfloat16), "tensor").astype(jnp.float32)
    attn_rows = lax.dynamic_slice_in_dim(summed_all, lax.axis_index("tensor") * tok_dev, tok_dev, 0)
    stream = resid.astype(jnp.float32) + attn_rows
    mean_square = jnp.mean(stream * stream, axis=1, keepdims=True)
    normed = (stream * lax.rsqrt(mean_square + 1e-06) * norm_gain).astype(jnp.bfloat16)
    experts = lax.axis_size("dp") * lax.axis_size("tensor")
    top_count = routes.shape[1]
    capacity = 2 * tok_dev * top_count // experts
    d_model = normed.shape[1]
    hidden_units = expert_down.shape[1]
    flat_ids = routes.reshape(-1)
    onehot = (flat_ids[:, None] == jnp.arange(experts, dtype=jnp.int32)[None, :]).astype(jnp.int32)
    slot_rank = jnp.sum(onehot * (jnp.cumsum(onehot, axis=0) - 1), axis=1)
    slot_index = flat_ids * capacity + slot_rank
    slot_ids = jnp.arange(experts * capacity, dtype=jnp.int32)
    placing = jnp.any(
        slot_ids[:, None, None] == slot_index.reshape(tok_dev, top_count)[None], axis=2
    )
    outgoing = jnp.dot(placing.astype(jnp.bfloat16), normed, preferred_element_type=jnp.float32)
    outgoing = outgoing.astype(jnp.bfloat16).reshape(experts, capacity, d_model)
    row_block = lax.all_to_all(outgoing, ("dp", "tensor"), split_axis=0, concat_axis=0, tiled=True)
    row_shape = row_block.shape
    flat_rows = row_block.reshape(-1, row_shape[-1])
    joint_proj = jnp.dot(flat_rows, expert_in[0], preferred_element_type=jnp.float32)
    hidden = (jax.nn.silu(joint_proj[:, :hidden_units]) * joint_proj[:, hidden_units:]).astype(
        jnp.bfloat16
    )
    expert_out = jnp.dot(hidden, expert_down[0], preferred_element_type=jnp.float32).astype(
        jnp.bfloat16
    )
    returned = lax.all_to_all(
        expert_out.reshape(row_shape), ("dp", "tensor"), split_axis=0, concat_axis=0, tiled=True
    )
    results = returned.reshape(experts * capacity, d_model)
    picked = results[slot_index].reshape(tok_dev, top_count, d_model)
    routed_sum = jnp.einsum("tk,tkd->td", route_weights, picked.astype(jnp.float32))
    return (stream + routed_sum).astype(jnp.bfloat16)


def solution(mesh):
    return jax.shard_map(
        shards,
        mesh=mesh,
        in_specs=(
            P("dp", "tensor"),
            P("dp", "tensor", None),
            P("dp"),
            P("tensor", None, None),
            P("tensor", "dp"),
            P(("dp", "tensor"), None),
            P(),
            P(("dp", "tensor"), None),
            P(("dp", "tensor"), None),
            P(("dp", "tensor"), None, None),
            P(("dp", "tensor"), None, None),
        ),
        out_specs=P(("dp", "tensor"), None),
        check_vma=False,
    )
```

profile of v0, /device:TPU:1, one launch (start us, length us, event | category | flops | bytes accessed | tf_op | source)
XLA Modules:
  0.0 396.2 jit_solution(15991651440541174260)
XLA Ops:
  6.5 0.7 all-gather.3.cloned.1.call-update
  8.7 1.3 iota_compare_fusion
  10.0 4.3 %copy.35 = bf16[512,2304]{0,1:T(8,128)(2,1)} copy(bf16[512,2304]{1,0:T(8,128)(2,1)} %param.11) | data formatting | bytes 4718592 | tf_op args[0]
  14.3 48.7 %all-gather.3.cloned.1.call-done = bf16[1,3072,576]{2,1,0:T(8,128)(2,1)} async-done(((bf16[1,192,576]{2,1,0:T(8,128)(2,1)}), bf16[1,3072,576]{2,1,0:T(8,128)(2,1)}) %all-gather.3.cloned.1.call-update) | async-done | bytes 3538960 | tf_op jit(solution)/shard_map/all_gather | solution.py:29
  63.0 18.4 %fusion = (f32[4,512]{1,0:T(4,128)S(1)}, f32[3072,512,4]{1,0,2:T(8,128)}) fusion(pred[512,3072]{0,1:T(8,128)(4,1)S(1)} %iota_compare_fusion, bf16[512,4,576]{0,2,1:T(8,128)(2,1)} %bitcast.61, bf16[1,3072,576]{2,1,0:T(8,128)(2,1)} %all-gather.3.cloned.1.call-done), kind=kOutput, calls=%fused_computation.3 | convolution fusion | flops 7266629632 | bytes 32645120 | tf_op jit(solution)/shard_map/thc,kc->htk/dot_general | solution.py:32
  81.4 6.1 %copy.34 = bf16[1,3072,576]{1,2,0:T(8,128)(2,1)} copy(bf16[1,3072,576]{2,1,0:T(8,128)(2,1)} %all-gather.3.cloned.1.call-done) | data formatting | bytes 7077888 | tf_op jit(solution)/shard_map/all_gather | solution.py:29
  87.5 11.7 %fusion.1 = f32[4,512]{1,0:T(4,128)S(1)} fusion(f32[3072,512,4]{1,0,2:T(8,128)} %get-tuple-element.8, f32[4,512]{1,0:T(4,128)S(1)} %broadcast_maximum_fusion, pred[512,3072]{0,1:T(8,128)(4,1)S(1)} %iota_compare_fusion), kind=kLoop, calls=%fused_computation.4 | loop fusion | flops 31455232 | bytes 26755072 | tf_op jit(solution)/shard_map/reduce_sum | solution.py:40
  99.2 14.4 %fusion.5 = f32[4,512,512]{2,1,0:T(8,128)} fusion(f32[3072,512,4]{1,0,2:T(8,128)} %get-tuple-element.8, f32[4,512]{1,0:T(4,128)S(1)} %broadcast_maximum_fusion, pred[512,3072]{0,1:T(8,128)(4,1)S(1)} %iota_compare_fusion, bf16[3072,576]{0,1:T(8,128)(2,1)} %bitcast.60), kind=kOutput, calls=%fused_computation.8 | convolution fusion | flops 6473908224 | bytes 34086912 | tf_op jit(solution)/shard_map/htk,kc->htc/dot_general | solution.py:41
  113.7 3.1 fusion.19
  116.8 6.0 %convolution_convert_fusion.1 = bf16[512,3584]{1,0:T(8,128)(2,1)} fusion(bf16[512,512]{0,1:T(8,128)(2,1)S(1)} %bitcast.65, bf16[512,3584]{0,1:T(8,128)(2,1)} %all-gather.5.cloned.1.call-done), kind=kOutput, calls=%fused_computation.15 | convolution fusion | flops 1880883200 | bytes 7864320 | tf_op jit(solution)/shard_map/dot_general | solution.py:51
  124.1 97.0 %all-reduce.2.cloned.1.call-done = bf16[512,3584]{1,0:T(8,128)(2,1)} async-done(((bf16[512,3584]{1,0:T(8,128)(2,1)}), bf16[512,3584]{1,0:T(8,128)(2,1)}) %all-reduce.2.cloned.1.call-update) | async-done | bytes 3670032 | tf_op jit(solution)/shard_map/psum | solution.py:57
  221.1 1.1 multiply_reduce_fusion
  222.3 4.0 %convolution_convert_fusion = bf16[512,3584]{1,0:T(8,128)(2,1)} fusion(pred[512,32]{0,1:T(8,128)(4,1)S(1)} %fusion.22, bf16[32,3584]{1,0:T(8,128)(2,1)S(1)} %copy-done.2, f32[3584]{0:T(1024)S(1)} %copy-done.3, f32[32]{0:T(128)S(1)} %add_rsqrt_fusion, bf16[512,3584]{1,0:T(8,128)(2,1)} %all-reduce.2.cloned.1.call-done, s32[]{:T(128)S(6)} %select_n.22), kind=kOutput, calls=%fused_computation.14 | convolution fusion | flops 119963648 | bytes 4159620 | tf_op jit(solution)/shard_map/dot_general | solution.py:75
  226.3 7.0 %reshape.114 = bf16[128,4,3584]{2,1,0:T(4,128)(2,1)} reshape(bf16[512,3584]{1,0:T(8,128)(2,1)} %convolution_convert_fusion) | data formatting | bytes 7340032 | tf_op jit(solution)/shard_map/reshape | solution.py:76
  233.3 55.2 %all_to_all.10 = bf16[128,4,3584]{2,1,0:T(4,128)(2,1)} all-to-all(bf16[128,4,3584]{2,1,0:T(4,128)(2,1)} %reshape.114), channel_id=1, replica_groups=mesh['dp'=8,'tensor'=16] {'dp','tensor'}, dimensions={0} | all-to-all | bytes 7340032 | tf_op jit(solution)/shard_map/all_to_all | solution.py:77
  288.5 6.7 %reshape.115 = bf16[512,3584]{1,0:T(8,128)(2,1)} reshape(bf16[128,4,3584]{2,1,0:T(4,128)(2,1)} %all_to_all.10) | data formatting | bytes 7340032 | tf_op jit(solution)/shard_map/reshape | solution.py:79
  295.3 12.1 %fusion.3 = f32[512,2048]{1,0:T(8,128)S(1)} fusion(bf16[512,3584]{1,0:T(8,128)(2,1)} %reshape.115, bf16[1,3584,2048]{2,1,0:T(8,128)(2,1)} %param.20), kind=kOutput, calls=%fused_computation.6 | convolution fusion | flops 7516192768 | bytes 22544384 | tf_op jit(solution)/shard_map/dot_general | solution.py:80
  307.3 8.7 %fusion.10 = bf16[512,3584]{1,0:T(8,128)(2,1)} fusion(bf16[1,1024,3584]{2,1,0:T(8,128)(2,1)} %param.21, f32[512,2048]{1,0:T(8,128)S(1)} %fusion.3), kind=kOutput, calls=%fused_computation.13 | convolution fusion | flops 3763077120 | bytes 15204352 | tf_op jit(solution)/shard_map/dot_general | solution.py:84
  316.0 7.0 %reshape.116 = bf16[128,4,3584]{2,1,0:T(4,128)(2,1)} reshape(bf16[512,3584]{1,0:T(8,128)(2,1)} %fusion.10) | data formatting | bytes 7340032 | tf_op jit(solution)/shard_map/reshape | solution.py:88
  323.0 5.0 %all-to-all-start.1 = ((bf16[128,4,3584]{2,1,0:T(4,128)(2,1)}), bf16[128,4,3584]{2,1,0:T(4,128)(2,1)}, u32[]{:S(2)}, u32[]{:S(2)}) async-start(bf16[128,4,3584]{2,1,0:T(4,128)(2,1)} %reshape.116), calls=%async_computation.1 | async-start | bytes 7340032 | tf_op jit(solution)/shard_map/all_to_all | solution.py:87
  328.3 46.2 %all-to-all-done.1 = bf16[128,4,3584]{2,1,0:T(4,128)(2,1)} async-done(((bf16[128,4,3584]{2,1,0:T(4,128)(2,1)}), bf16[128,4,3584]{2,1,0:T(4,128)(2,1)}, u32[]{:S(2)}, u32[]{:S(2)}) %all-to-all-start.1) | async-done | bytes 3670048 | tf_op jit(solution)/shard_map/all_to_all | solution.py:87
  374.5 6.7 %reshape.117 = bf16[512,3584]{1,0:T(8,128)(2,1)} reshape(bf16[128,4,3584]{2,1,0:T(4,128)(2,1)} %all-to-all-done.1) | data formatting | bytes 7340032 | tf_op jit(solution)/shard_map/reshape | solution.py:90
  381.3 6.1 %gather_fusion = bf16[256,3584]{1,0:T(8,128)(2,1)S(1)} fusion(bf16[512,3584]{1,0:T(8,128)(2,1)} %reshape.117, s32[1024]{0:T(1024)S(1)} %pad_clamp_fusion), kind=kCustom, calls=%fused_computation | custom fusion | bytes 3671040 | tf_op jit(solution)/shard_map/gather | solution.py:91
  388.0 1.7 fusion.23
  (40 shorter events, 2.8 us)
Async XLA Ops:
  6.5 107.1 %copy-start = (bf16[4,512,128]{2,1,0:T(8,128)(2,1)S(1)}, bf16[4,512,128]{2,1,0:T(8,128)(2,1)}, u32[]{:S(2)}) copy-start(bf16[4,512,128]{2,1,0:T(8,128)(2,1)} %param.14) | copy-start | bytes 1572868
  6.5 56.5 %all-gather.3.cloned.1.call-start = ((), (), s32[]{:S(2)}) async-start(), calls=%async_computation.2 | async-start | bytes 4177920 | tf_op jit(solution)/shard_map/all_gather | solution.py:29
  7.3 109.5 %all-gather.5.cloned.1.call-start = ((), (), s32[]{:S(2)}) async-start(), calls=%async_computation.3 | async-start | bytes 4128768 | tf_op jit(solution)/shard_map/all_gather | solution.py:53
  8.0 213.1 %all-reduce.2.cloned.1.call-start = ((), (), s32[]{:S(2)}) async-start(), calls=%async_computation.4 | async-start | bytes 7340032 | tf_op jit(solution)/shard_map/psum | solution.py:57
  116.8 6.1 %copy-start.4 = (s32[32,8]{0,1:T(8,128)S(1)}, s32[32,8]{0,1:T(8,128)}, u32[]{:S(2)}) copy-start(s32[32,8]{0,1:T(8,128)} %param.18) | copy-start | bytes 3076
  122.8 98.3 %copy-start.2 = (bf16[32,3584]{1,0:T(8,128)(2,1)S(1)}, bf16[32,3584]{1,0:T(8,128)(2,1)}, u32[]{:S(2)}) copy-start(bf16[32,3584]{1,0:T(8,128)(2,1)} %param.16) | copy-start | bytes 688132
  122.8 99.5 %copy-start.3 = (f32[3584]{0:T(1024)S(1)}, f32[3584]{0:T(1024)}, u32[]{:S(2)}) copy-start(f32[3584]{0:T(1024)} %param.17) | copy-start | bytes 43012
  323.0 5.1 %copy-start.5 = (f32[32,8]{0,1:T(8,128)S(1)}, f32[32,8]{0,1:T(8,128)}, u32[]{:S(2)}) copy-start(f32[32,8]{0,1:T(8,128)} %param.19) | copy-start | bytes 3076
  323.0 51.5 %all-to-all-start.1 = ((bf16[128,4,3584]{2,1,0:T(4,128)(2,1)}), bf16[128,4,3584]{2,1,0:T(4,128)(2,1)}, u32[]{:S(2)}, u32[]{:S(2)}) async-start(bf16[128,4,3584]{2,1,0:T(4,128)(2,1)} %reshape.116), calls=%async_computation.1 | async-start | bytes 7340032 | tf_op jit(solution)/shard_map/all_to_all | solution.py:87
  381.3 8.4 %copy-start.1 = (bf16[4,512,128]{2,1,0:T(8,128)(2,1)S(1)}, bf16[4,512,128]{2,1,0:T(8,128)(2,1)}, u32[]{:S(2)}) copy-start(bf16[4,512,128]{2,1,0:T(8,128)(2,1)} %param.14) | copy-start | bytes 1572868
Sparse Core Ops, SparseCore 0:
  9.5 53.4 all-gather.2
  64.7 30.2 all-gather.4
  123.0 98.1 all-reduce.1
where the time goes:
time: 398 us; the launch traced here: 396 us
  waiting for transfers between devices  193 us (48%)
  matrix products  67.3 us (17%)
  blocking collectives  55.2 us (14%)
  local copies, waits for them, and re-layouts  44.7 us (11%)
  other arithmetic  16.6 us (4%)
  between operations  13.9 us (3%)
  starting transfers between devices  5.11 us (1%)
    psum x1, waiting for transfers between devices, shards(): lax.psum(partial_value.astype(jnp.bfloat16), 'tensor').astype(jnp.float32)  97 us
    all_to_all x1, blocking collectives, shards(): lax.all_to_all(outgoing, ('dp', 'tensor'), split_axis=0, concat_axis=0, t...  55.2 us
    all_gather x1, waiting for transfers between devices, shards(): key_rows = lax.all_gather(cache, 'tensor', axis=1, tiled=True)[0]  48.7 us
    all_to_all x1, waiting for transfers between devices, shards(): lax.all_to_all(expert_out.reshape(row_shape), ('dp', 'tensor'), split_axi...  46.2 us
    dot_general x1, matrix products, shards(): jnp.einsum('thc,kc->htk', query_heads, key_rows, preferred_element_type=j...  18.4 us
    dot_general x1, matrix products, shards(): jnp.einsum('htk,kc->htc', weights.astype(jnp.bfloat16), key_rows[:, :late...  14.4 us
    dot_general x1, matrix products, shards(): jnp.dot(flat_rows, expert_in[0], preferred_element_type=jnp.float32)  12.1 us
    reduce_sum x1, other arithmetic, shards(): totals = jnp.sum(weights, axis=2)  11.7 us
  transfers between devices with their start and end apart: 4, of which 3 were waited for; matrix products, arithmetic and copies ran while one was open for 15% of the time, Pallas kernels for 0%

commit v1 on v0

v1 whole, which is shorter than its diff:
```python
import functools

import jax
import jax.numpy as jnp
from jax import lax
from jax.experimental import pallas as pl
from jax.experimental.pallas import tpu as pltpu
from jax.sharding import PartitionSpec as P

MESH = pl.DeviceIdType.MESH
BF16, F32, I32 = jnp.bfloat16, jnp.float32, jnp.int32
NEAR = (
    (1, 0), (0, 1), (3, 0), (0, 3), (1, 1), (3, 3), (1, 3), (3, 1),
    (2, 0), (0, 2), (2, 2), (2, 1), (1, 2), (2, 3), (3, 2),
)
ROUNDS = (
    ((0, 0, 640), (1, 640, 640), (2, 1280, 512)),
    ((0, 1792, 640), (1, 2432, 512), (2, 2944, 640)),
)


def whole(ref, sem):
    pltpu.make_async_copy(ref, ref, sem).wait()


def dot(a, b):
    return jnp.dot(a, b, preferred_element_type=F32)


class Place:
    def __init__(self):
        dp, t = lax.axis_index("dp"), lax.axis_index("tensor")
        self.z, self.c = lax.div(dp, 2), lax.rem(dp, 2)
        self.x, self.y = lax.div(t, 4), lax.rem(t, 4)

    def line(self, part, a, core):
        if part == 0:
            return (a * 2 + core, self.x * 4 + self.y)
        if part == 1:
            return (self.z * 2 + core, a * 4 + self.y)
        return (self.z * 2 + core, self.x * 4 + a)

    def own_line(self, part):
        return (self.z, self.x, self.y)[part]

    def plane(self, part, b1, b2):
        if part == 0:
            return (self.z * 2 + self.c, b1 * 4 + b2)
        if part == 1:
            return (b1 * 2 + self.c, self.x * 4 + b2)
        return (b2 * 2 + self.c, b1 * 4 + self.y)

    def own_plane(self, part):
        return ((self.x, self.y), (self.z, self.y), (self.x, self.z))[part]

    def expert(self, part, j):
        b1, b2 = j // 4, j % 4
        if part == 0:
            return (self.z * 2 + self.c) * 16 + j
        if part == 1:
            return (b1 * 2 + self.c) * 16 + self.x * 4 + b2
        return (b2 * 2 + self.c) * 16 + b1 * 4 + self.y


def up(v, n):
    return lax.rem(v + n, 4)


def partners(me):
    out = [(me.z * 2 + 1 - me.c, me.x * 4 + me.y)]
    for part in range(3):
        for n in (1, 2, 3):
            out.append(me.line(part, up(me.own_line(part), n), 1 - me.c))
    for dz in range(4):
        for dx in range(4):
            for dy in range(4):
                if (dz, dx, dy) != (0, 0, 0) and 0 in (dz, dx, dy):
                    out.append((up(me.z, dz) * 2 + me.c, up(me.x, dx) * 4 + up(me.y, dy)))
    return out


def back_kernel(
    ho_ref, wo_ref, resid_ref, gain_ref, meta_ref, win_hbm, wdown_hbm,
    out_ref,
    win, wdown, part4, r1, l1, r2, l2, mid, r1b, l1b, r2b, l2b,
    metas, pick, wgt, swap, stream, nrm, toks, outg, rows, stage, acc, hid, psum, recv,
    wsem, rs_s, rs_r, m_s, m_r, g_s, g_r, d_s, d_r, t_s, t_r, c_s, c_r,
):
    me = Place()
    loads = [
        pltpu.make_async_copy(win_hbm.at[pl.ds(0, 1792)], win.at[pl.ds(0, 1792)], wsem.at[0]),
        pltpu.make_async_copy(win_hbm.at[pl.ds(1792, 1792)], win.at[pl.ds(1792, 1792)], wsem.at[1]),
        pltpu.make_async_copy(wdown_hbm, wdown, wsem.at[2]),
    ]
    for load in loads:
        load.start()

    barrier = pltpu.get_barrier_semaphore()
    others = partners(me)
    for other in others:
        pl.semaphore_signal(barrier, inc=1, device_id=other, device_id_type=MESH)
    pl.semaphore_wait(barrier, len(others))

    def send(src, dst, ssem, rsem, device):
        copy = pltpu.make_async_remote_copy(
            src_ref=src, dst_ref=dst, send_sem=ssem, recv_sem=rsem,
            device_id=device, device_id_type=MESH,
        )
        copy.start()
        return copy

    def half_cols(h):
        return pl.ds(h * 1792, 1792)

    def group(h, k, lo, n):
        cols = pl.ds(h * 1792 + lo, n)
        return part4.at[k, :, :, cols] if h == 0 else part4.at[:, k, :, cols]

    def project(h, k):
        head = ho_ref[k] if h == 0 else ho_ref[:, k]
        value = dot(head.reshape(128, 512), wo_ref[:, half_cols(h)])
        group(h, k, 0, 1792)[...] = value.astype(BF16).reshape(4, 32, 1792)

    def neighbour(h, phase, n):
        along_x = (h == 0) == (phase == 0)
        if along_x:
            return (me.z * 2 + me.c, up(me.x, n) * 4 + me.y)
        return (me.z * 2 + me.c, me.x * 4 + up(me.y, n))

    def position(h, phase):
        return me.x if (h == 0) == (phase == 0) else me.y

    def piece(h, phase, k, lo, n):
        return group(h, k, lo, n) if phase == 0 else mid.at[h, k, :, pl.ds(lo, n)]

    def boxes(phase):
        return (r1, l1, r2, l2) if phase == 0 else (r1b, l1b, r2b, l2b)

    def box(ref, h, phase, lo, n):
        if phase == 0:
            return ref.at[h, :, :, pl.ds(lo, n)]
        return ref.at[h, :, pl.ds(lo, n)]

    started = {}

    def first_far(h, phase):
        k = up(position(h, phase), 2)
        br1, bl1, _, _ = boxes(phase)
        for side, (ref, lo, n) in enumerate(((br1, 0, 1), (bl1, 896, 3))):
            i = (h * 2 + phase) * 6 + side
            started[h, phase, side] = send(
                piece(h, phase, k, lo, 896), box(ref, h, phase, 0, 896),
                rs_s.at[i], rs_r.at[i], neighbour(h, phase, n),
            )

    def first_near(h, phase):
        _, _, br2, bl2 = boxes(phase)
        for side, (ref, lo, n) in enumerate(((br2, 896, 1), (bl2, 0, 3))):
            i = (h * 2 + phase) * 6 + 2 + side
            started[h, phase, 2 + side] = send(
                piece(h, phase, up(position(h, phase), n), lo, 896), box(ref, h, phase, lo, 896),
                rs_s.at[i], rs_r.at[i], neighbour(h, phase, n),
            )

    def second(h, phase):
        br1, bl1, br2, bl2 = boxes(phase)
        for side, (ref, to, lo, n) in enumerate(((br1, br2, 0, 1), (bl1, bl2, 896, 3))):
            i = (h * 2 + phase) * 6 + 4 + side
            started[h, phase, side].wait_recv()
            mine = piece(h, phase, up(position(h, phase), n), lo, 896)
            mine[...] = (mine[...].astype(F32) + box(ref, h, phase, 0, 896)[...].astype(F32)).astype(BF16)
            started[h, phase, 4 + side] = send(
                mine, box(to, h, phase, lo, 896), rs_s.at[i], rs_r.at[i], neighbour(h, phase, n)
            )

    def last(h, phase):
        for i in (2, 3, 4, 5):
            started[h, phase, i].wait_recv()
        _, _, br2, bl2 = boxes(phase)
        total = piece(h, phase, position(h, phase), 0, 1792)[...].astype(F32)
        total += box(br2, h, phase, 0, 1792)[...].astype(F32)
        return total + box(bl2, h, phase, 0, 1792)[...].astype(F32)

    meta_sends = []
    for part in range(3):
        own = me.own_line(part) * 2 + me.c
        for n in range(4):
            for core in range(2):
                if (n, core) == (0, 0):
                    continue
                to = me.line(part, up(me.own_line(part), n), lax.rem(me.c + core, 2))
                meta_sends.append(send(meta_ref, metas.at[part, own], m_s.at[part], m_r.at[part], to))
        pltpu.make_async_copy(meta_ref, metas.at[part, own], m_r.at[part]).start()

    for h in range(2):
        project(h, up(position(h, 0), 2))
    for h in range(2):
        first_far(h, 0)
    for n in (1, 3):
        for h in range(2):
            project(h, up(position(h, 0), n))
    for h in range(2):
        first_near(h, 0)
    for h in range(2):
        project(h, position(h, 0))

    token = lax.broadcasted_iota(I32, (256, 256), 0)
    other = lax.broadcasted_iota(I32, (256, 256), 1)
    earlier = jnp.where((token // 32 == other // 32) & (other < token), 1.0, 0.0).astype(BF16)
    lane = lax.broadcasted_iota(I32, (128, 512), 1)
    spread = jnp.where(lane // 32 == lax.broadcasted_iota(I32, (128, 512), 0), 1.0, 0.0).astype(BF16)
    slot = lax.broadcasted_iota(I32, (256, 512), 1) % 32
    of_source = slot // 4 == lax.broadcasted_iota(I32, (256, 512), 0) // 32
    rank_wanted = (slot % 4).astype(F32)
    for part in range(3):
        whole(metas.at[part], m_r.at[part])
        table = metas[part].reshape(256, 128)
        column = lax.broadcasted_iota(I32, (256, 128), 1)
        wanted = jnp.where(column < 16, me.expert(part, column), -1).astype(F32)
        hit = jnp.zeros((256, 128), F32)
        weight = jnp.zeros((256, 128), F32)
        for k in range(8):
            same = table[:, k : k + 1] == wanted
            hit = jnp.where(same, 1.0, hit)
            weight = jnp.where(same, table[:, 8 + k : 9 + k], weight)
        rank = dot(earlier, hit.astype(BF16))
        rank = jnp.where(hit > 0.5, rank, -1.0)
        chosen = (dot(rank.astype(BF16), spread) == rank_wanted) & of_source
        pick[part] = jnp.where(chosen, 1.0, 0.0).T.astype(BF16)
        wgt[part] = jnp.where(chosen, dot(weight.astype(BF16), spread), 0.0).astype(BF16)
    row = lax.broadcasted_iota(I32, (512, 512), 0)
    col = lax.broadcasted_iota(I32, (512, 512), 1)
    rx, ry, rz, low = row // 128, (row // 32) % 4, (row // 8) % 4, row % 8
    swap[0] = jnp.where(col == rz * 128 + ry * 32 + rx * 8 + low, 1.0, 0.0).astype(BF16)
    swap[1] = jnp.where(col == rx * 128 + rz * 32 + ry * 8 + low, 1.0, 0.0).astype(BF16)

    for h in range(2):
        second(h, 0)
    for h in range(2):
        mid[h] = last(h, 0).astype(BF16)
    for h in range(2):
        first_far(h, 1)
    for h in range(2):
        first_near(h, 1)
    for h in range(2):
        second(h, 1)
    for h in range(2):
        stream[:, half_cols(h)] = last(h, 1) + resid_ref[:, half_cols(h)].astype(F32)
    value = stream[...]
    mean_square = jnp.mean(value * value, axis=1, keepdims=True)
    nrm[...] = (value * lax.rsqrt(mean_square + 1e-06) * gain_ref[...]).astype(BF16)
    for copy in started.values():
        copy.wait_send()

    def gather(i):
        for p, (part, lo, n) in enumerate(ROUNDS[i]):
            own = me.own_line(part) * 2 + me.c
            at = i * 3 + p
            for step, core in ((0, 1), (1, 0), (3, 0), (1, 1), (3, 1), (2, 0), (2, 1)):
                to = me.line(part, up(me.own_line(part), step), lax.rem(me.c + core, 2))
                send(nrm.at[:, pl.ds(lo, n)], toks.at[own, :, pl.ds(lo, n)], g_s.at[at], g_r.at[at], to)
            pltpu.make_async_copy(nrm.at[:, pl.ds(lo, n)], toks.at[own, :, pl.ds(lo, n)], g_r.at[at]).start()

    def flat(ref, lo, n):
        return ref[:, :, :, pl.ds(lo, n)].reshape(512, n)

    def exchange(i, src, dst_of, ssem, rsem):
        for d1, d2 in NEAR:
            for p, (part, lo, n) in enumerate(ROUNDS[i]):
                b1, b2 = me.own_plane(part)
                e1, e2 = up(b1, d1), up(b2, d2)
                send(
                    src.at[e1, e2, :, pl.ds(lo, n)], dst_of(part).at[b1, b2, :, pl.ds(lo, n)],
                    ssem.at[i * 3 + p], rsem.at[i * 3 + p], me.plane(part, e1, e2),
                )
        for p, (part, lo, n) in enumerate(ROUNDS[i]):
            b1, b2 = me.own_plane(part)
            pltpu.make_async_copy(
                src.at[b1, b2, :, pl.ds(lo, n)], dst_of(part).at[b1, b2, :, pl.ds(lo, n)],
                rsem.at[i * 3 + p],
            ).start()

    def landing(part):
        return rows if part == 0 else stage

    def block(ref, lo, n):
        return ref.at[:, :, :, pl.ds(lo, n)]

    def sent(ref, lo, n, sem):
        for k in range(3):
            whole(ref.at[k, :, :, pl.ds(lo, n)], sem)
        whole(ref.at[3, pl.ds(0, 3), :, pl.ds(lo, n)], sem)

    def dispatch(i):
        for p, (part, lo, n) in enumerate(ROUNDS[i]):
            whole(toks.at[:, :, pl.ds(lo, n)], g_r.at[i * 3 + p])
            value = dot(pick[part], toks[:, :, pl.ds(lo, n)].reshape(256, n))
            outg[:, :, :, pl.ds(lo, n)] = value.astype(BF16).reshape(4, 4, 32, n)
        exchange(i, outg, landing, d_s, d_r)

    def arrive(i):
        for p, (part, lo, n) in enumerate(ROUNDS[i]):
            whole(block(landing(part), lo, n), d_r.at[i * 3 + p])
            if part:
                value = dot(swap[part - 1], flat(stage, lo, n))
                rows[:, :, :, pl.ds(lo, n)] = value.astype(BF16).reshape(4, 4, 32, n)

    gather(0)
    gather(1)
    dispatch(0)
    dispatch(1)

    loads[0].wait()
    arrive(0)

    def first_half(j, carry):
        cols = pl.ds(pl.multiple_of(j * 256, 256), 256)
        acc[:, cols] = dot(flat(rows, 0, 1792), win[pl.ds(0, 1792), cols])
        return carry

    lax.fori_loop(0, 8, first_half, 0)
    loads[1].wait()
    arrive(1)

    def second_half(j, carry):
        cols = pl.ds(pl.multiple_of(j * 256, 256), 256)
        more = pl.ds(pl.multiple_of(j * 256 + 1024, 256), 256)
        gate = acc[:, cols] + dot(flat(rows, 1792, 1792), win[pl.ds(1792, 1792), cols])
        lift = acc[:, more] + dot(flat(rows, 1792, 1792), win[pl.ds(1792, 1792), more])
        hid[0, :, cols] = (gate / (1.0 + jnp.exp(-gate)) * lift).astype(BF16)
        return carry

    lax.fori_loop(0, 4, second_half, 0)
    loads[2].wait()
    for part in (1, 2):
        hid[part] = dot(swap[part - 1], hid[0]).astype(BF16)
    for i in range(2):
        for p, (part, lo, n) in enumerate(ROUNDS[i]):
            sent(outg, lo, n, d_s.at[i * 3 + p])
            whole_gather = toks.at[pl.ds(0, 7), :, pl.ds(lo, n)]
            whole(whole_gather, g_s.at[i * 3 + p])
            value = dot(hid[part], wdown[:, pl.ds(lo, n)])
            outg[:, :, :, pl.ds(lo, n)] = value.astype(BF16).reshape(4, 4, 32, n)
        exchange(i, outg, lambda part: part4, t_s, t_r)

    for i in range(2):
        for p, (part, lo, n) in enumerate(ROUNDS[i]):
            at = i * 3 + p
            whole(block(part4, lo, n), t_r.at[at])
            value = dot(wgt[part], flat(part4, lo, n))
            psum[:, :, pl.ds(lo, n)] = value.astype(BF16).reshape(8, 32, n)
            own = me.own_line(part) * 2 + me.c
            for step, core in ((0, 1), (1, 0), (3, 0), (1, 1), (3, 1), (2, 0), (2, 1)):
                a, k = up(me.own_line(part), step), lax.rem(me.c + core, 2)
                send(
                    psum.at[a * 2 + k, :, pl.ds(lo, n)], recv.at[own, :, pl.ds(lo, n)],
                    c_s.at[at], c_r.at[at], me.line(part, a, k),
                )
            pltpu.make_async_copy(
                psum.at[own, :, pl.ds(lo, n)], recv.at[own, :, pl.ds(lo, n)], c_r.at[at]
            ).start()
    for i in range(2):
        for p, (part, lo, n) in enumerate(ROUNDS[i]):
            at = i * 3 + p
            whole(recv.at[:, :, pl.ds(lo, n)], c_r.at[at])
            total = stream[:, pl.ds(lo, n)]
            for q in range(8):
                total += recv[q, :, pl.ds(lo, n)].astype(F32)
            out_ref[:, pl.ds(lo, n)] = total.astype(BF16)
    for i in range(2):
        for p, (part, lo, n) in enumerate(ROUNDS[i]):
            at = i * 3 + p
            sent(outg, lo, n, t_s.at[at])
            whole(psum.at[pl.ds(0, 7), :, pl.ds(lo, n)], c_s.at[at])
    for part in range(3):
        whole(metas.at[part, pl.ds(0, 7)], m_s.at[part])


def back(head_out, out_proj, resid, norm_gain, meta, expert_in, expert_down):
    vmem = pl.BlockSpec(memory_space=pltpu.VMEM)
    hbm = pl.BlockSpec(memory_space=pl.ANY)
    dma = pltpu.SemaphoreType.DMA
    grid_rows = (4, 4, 32, 3584)
    return pl.pallas_call(
        back_kernel,
        out_shape=jax.ShapeDtypeStruct((32, 3584), BF16),
        in_specs=[vmem, vmem, vmem, vmem, vmem, hbm, hbm],
        out_specs=vmem,
        scratch_shapes=[
            pltpu.VMEM((3584, 2048), BF16),
            pltpu.VMEM((1024, 3584), BF16),
            pltpu.VMEM(grid_rows, BF16),
            pltpu.VMEM((2, 4, 32, 896), BF16),
            pltpu.VMEM((2, 4, 32, 896), BF16),
            pltpu.VMEM((2, 4, 32, 1792), BF16),
            pltpu.VMEM((2, 4, 32, 1792), BF16),
            pltpu.VMEM((2, 4, 32, 1792), BF16),
            pltpu.VMEM((2, 32, 896), BF16),
            pltpu.VMEM((2, 32, 896), BF16),
            pltpu.VMEM((2, 32, 1792), BF16),
            pltpu.VMEM((2, 32, 1792), BF16),
            pltpu.VMEM((3, 8, 32, 128), F32),
            pltpu.VMEM((3, 512, 256), BF16),
            pltpu.VMEM((3, 256, 512), BF16),
            pltpu.VMEM((2, 512, 512), BF16),
            pltpu.VMEM((32, 3584), F32),
            pltpu.VMEM((32, 3584), BF16),
            pltpu.VMEM((8, 32, 3584), BF16),
            pltpu.VMEM(grid_rows, BF16),
            pltpu.VMEM(grid_rows, BF16),
            pltpu.VMEM(grid_rows, BF16),
            pltpu.VMEM((512, 2048), F32),
            pltpu.VMEM((3, 512, 1024), BF16),
            pltpu.VMEM((8, 32, 3584), BF16),
            pltpu.VMEM((8, 32, 3584), BF16),
            dma((3,)),
            dma((24,)),
            dma((24,)),
            dma((3,)),
            dma((3,)),
            dma((6,)),
            dma((6,)),
            dma((6,)),
            dma((6,)),
            dma((6,)),
            dma((6,)),
            dma((6,)),
            dma((6,)),
        ],
        compiler_params=pltpu.CompilerParams(
            collective_id=1, has_side_effects=True, vmem_limit_bytes=67043328
        ),
        name="back",
    )(head_out, out_proj, resid, norm_gain, meta, expert_in, expert_down)


def shards(
    queries,
    cache,
    offsets,
    value_up,
    out_proj,
    resid,
    norm_gain,
    routes,
    route_weights,
    expert_in,
    expert_down,
):
    heads_dev = value_up.shape[0]
    latent_width = value_up.shape[1]
    key_width = cache.shape[2]
    tok_grp = queries.shape[0]
    score_scale = (value_up.shape[2] + key_width - latent_width) ** (-0.5)
    query_heads = queries.reshape(tok_grp, heads_dev, key_width)
    start_pos = offsets[0]
    query_pos = start_pos + jnp.arange(tok_grp, dtype=jnp.int32)
    key_rows = lax.all_gather(cache, "tensor", axis=1, tiled=True)[0]
    key_count = key_rows.shape[0]
    scores = (
        jnp.einsum("thc,kc->htk", query_heads, key_rows, preferred_element_type=jnp.float32)
        * score_scale
    )
    key_pos = jnp.arange(key_count, dtype=jnp.int32)
    visible = key_pos[None, :] <= query_pos[:, None]
    scores = jnp.where(visible[None], scores, jnp.float32(-1e30))
    highest = jnp.max(scores, axis=2)
    weights = jnp.where(visible[None], jnp.exp(scores - highest[..., None]), jnp.float32(0.0))
    totals = jnp.sum(weights, axis=2)
    weighted = jnp.einsum(
        "htk,kc->htc",
        weights.astype(jnp.bfloat16),
        key_rows[:, :latent_width],
        preferred_element_type=jnp.float32,
    )
    context = (weighted / totals[..., None]).astype(jnp.bfloat16)
    head_out = jnp.einsum("htc,hcv->thv", context, value_up, preferred_element_type=jnp.float32)
    head_out = head_out.astype(jnp.bfloat16).reshape(4, 4, 32, -1)
    wide = lax.all_gather(out_proj, "dp", axis=1, tiled=True)
    meta = jnp.concatenate([routes.astype(F32), route_weights], axis=1)
    meta = jnp.pad(meta, ((0, 0), (0, 112)))
    return back(head_out, wide, resid, norm_gain[None], meta, expert_in[0], expert_down[0])


def solution(mesh):
    return jax.shard_map(
        shards,
        mesh=mesh,
        in_specs=(
            P("dp", "tensor"),
            P("dp", "tensor", None),
            P("dp"),
            P("tensor", None, None),
            P("tensor", "dp"),
            P(("dp", "tensor"), None),
            P(),
            P(("dp", "tensor"), None),
            P(("dp", "tensor"), None),
            P(("dp", "tensor"), None, None),
            P(("dp", "tensor"), None, None),
        ),
        out_specs=P(("dp", "tensor"), None),
        check_vma=False,
    )
```

time: 398 us -> 282 us (0.71)
  waiting for transfers between devices: 193 us -> 72.6 us
  Pallas kernels: 0 us -> 120 us
  blocking collectives: 55.2 us -> 0 us
  matrix products: 67.3 us -> 27 us
  local copies, waits for them, and re-layouts: 44.7 us -> 19.5 us
  other arithmetic: 16.6 us -> 27.8 us
  starting transfers between devices: 5.11 us -> 0.04 us
    pallas_call x0 -> x1, Pallas kernels: none -> 120 us  [back(): pl.pallas_call(back_kernel, out_shape=jax.ShapeDtypeStruct((32, 3584), BF...]
    psum x1 -> x0, waiting for transfers between devices: 97 us -> none  [shards(): lax.psum(partial_value.astype(jnp.bfloat16), 'tensor').astype(jnp.float32)]
    all_to_all x1 -> x0, blocking collectives: 55.2 us -> none  [shards(): lax.all_to_all(outgoing, ('dp', 'tensor'), split_axis=0, concat_axis=0, t...]
    all_to_all x1 -> x0, waiting for transfers between devices: 46.2 us -> none  [shards(): lax.all_to_all(expert_out.reshape(row_shape), ('dp', 'tensor'), split_axi...]
    dot_general x6 -> x0, matrix products: 45.8 us -> none  [the longest x1 14.4 us: shards(): jnp.einsum('htk,kc->htc', weights.astype(jnp.bfloat16), key_rows[:, :late...]
    reshape x4 -> x1, local copies, waits for them, and re-layouts: 27.5 us -> 0.99 us  [shards(): head_out = head_out.astype(jnp.bfloat16).reshape(4, 4, 32, -1)]
    all_gather x1, waiting for transfers between devices: 0.02 us -> 25.3 us  [shards(): wide = lax.all_gather(out_proj, 'dp', axis=1, tiled=True)]
    sub x1, other arithmetic: 0.06 us -> 23.9 us  [shards(): scores - highest[..., None]]
  transfers between devices with their start and end apart: 4 -> 2, of which waited for: 3 -> 2; matrix products, arithmetic and copies ran while one was open for 15% -> 5% of each run, Pallas kernels for 0% -> 0%
where the time goes in v1:
time: 282 us; the launch traced here: 281 us
  Pallas kernels  120 us (43%)
  waiting for transfers between devices  72.6 us (26%)
  other arithmetic  27.8 us (10%)
  matrix products  27 us (10%)
  local copies, waits for them, and re-layouts  19.5 us (7%)
  between operations  14.1 us (5%)
    pallas_call x1, Pallas kernels, back(): pl.pallas_call(back_kernel, out_shape=jax.ShapeDtypeStruct((32, 3584), BF...  120 us
    all_gather x1, waiting for transfers between devices, shards(): key_rows = lax.all_gather(cache, 'tensor', axis=1, tiled=True)[0]  45.9 us
    all_gather x1, waiting for transfers between devices, shards(): wide = lax.all_gather(out_proj, 'dp', axis=1, tiled=True)  25.3 us
    sub x1, other arithmetic, shards(): scores - highest[..., None]  23.9 us
    dot_general x1, matrix products, shards(): jnp.einsum('thc,kc->htk', query_heads, key_rows, preferred_element_type=j...  15.7 us
    dot_general x1, matrix products, shards(): jnp.einsum('htc,hcv->thv', context, value_up, preferred_element_type=jnp....  11.4 us
    all_gather x1, local copies, waits for them, and re-layouts, shards(): wide = lax.all_gather(out_proj, 'dp', axis=1, tiled=True)  5.92 us
  transfers between devices with their start and end apart: 2, of which 2 were waited for; matrix products, arithmetic and copies ran while one was open for 5% of the time, Pallas kernels for 0%

profile of v1, /device:TPU:1, one launch (start us, length us, event | category | flops | bytes accessed | tf_op | source)
XLA Modules:
  0.0 281.2 jit_solution(6201230976464629221)
XLA Ops:
  6.5 0.0 all-gather.5.cloned.1.call-start
  6.5 0.7 all-gather.5.cloned.1.call-update
  7.3 0.0 all-gather.3.cloned.1.call-start
  7.3 0.7 all-gather.3.cloned.1.call-update
  8.0 2.8 %copy.33 = bf16[512,2304]{0,1:T(8,128)(2,1)S(1)} copy(bf16[512,2304]{1,0:T(8,128)(2,1)} %param.11) | data formatting | bytes 4718592 | tf_op args[0]
  11.5 1.3 broadcast_in_dim.30.gain_ref
  12.8 0.8 copy.38
  13.6 0.7 convert_element_type.21
  14.3 0.1 copy.37
  14.4 0.7 select_maximum_fusion.meta_ref
  15.0 2.5 iota_compare_fusion
  17.5 25.3 %all-gather.5.cloned.1.call-done = bf16[512,3584]{0,1:T(8,128)(2,1)} async-done(((bf16[512,448]{0,1:T(8,128)(2,1)}), bf16[512,3584]{0,1:T(8,128)(2,1)}) %all-gather.5.cloned.1.call-update) | async-done | bytes 3670032 | tf_op jit(solution)/shard_map/all_gather | solution.py:479
  42.9 5.9 %copy.39.wo_ref = bf16[512,3584]{1,0:T(8,128)(2,1)} copy(bf16[512,3584]{0,1:T(8,128)(2,1)} %all-gather.5.cloned.1.call-done) | data formatting | bytes 7340032 | tf_op jit(solution)/shard_map/all_gather | solution.py:479
  48.8 45.9 %all-gather.3.cloned.1.call-done = bf16[1,3072,576]{2,1,0:T(8,128)(2,1)} async-done(((bf16[1,192,576]{2,1,0:T(8,128)(2,1)}), bf16[1,3072,576]{2,1,0:T(8,128)(2,1)}) %all-gather.3.cloned.1.call-update) | async-done | bytes 3538960 | tf_op jit(solution)/shard_map/all_gather | solution.py:458
  94.6 0.0 copy-start
  94.6 15.7 %fusion.7 = f32[3072,512,4]{1,0,2:T(8,128)} fusion(bf16[512,4,576]{0,2,1:T(8,128)(2,1)S(1)} %bitcast.40, bf16[1,3072,576]{2,1,0:T(8,128)(2,1)} %all-gather.3.cloned.1.call-done), kind=kOutput, calls=%fused_computation.11 | convolution fusion | flops 7247757312 | bytes 31064064 | tf_op jit(solution)/shard_map/thc,kc->htk/dot_general | solution.py:461
  110.3 0.0 copy-done
  110.3 23.9 %fusion.22 = (f32[4,512]{1,0:T(4,128)S(1)}, bf16[4,512,3072]{1,2,0:T(8,128)(2,1)}) fusion(f32[3072,512,4]{1,0,2:T(8,128)} %fusion.7, pred[512,3072]{0,1:T(8,128)(4,1)S(1)} %copy-done), kind=kOutput, calls=%fused_computation.22 | output fusion | flops 50334720 | bytes 39329792 | tf_op jit(solution)/shard_map/sub | solution.py:468
  134.2 4.4 %copy.32 = bf16[1,3072,576]{1,2,0:T(8,128)(2,1)S(1)} copy(bf16[1,3072,576]{2,1,0:T(8,128)(2,1)} %all-gather.3.cloned.1.call-done) | data formatting | bytes 7077888 | tf_op jit(solution)/shard_map/all_gather | solution.py:458
  138.7 11.4 %fusion.17 = bf16[512,4,128]{2,0,1:T(8,128)(2,1)} fusion(bf16[4,512,128]{2,1,0:T(8,128)(2,1)} %param.14, bf16[3072,576]{0,1:T(8,128)(2,1)S(1)} %bitcast.39, bf16[4,512,3072]{1,2,0:T(8,128)(2,1)} %get-tuple-element.6, f32[4,512]{1,0:T(4,128)S(1)} %get-tuple-element.5), kind=kOutput, calls=%fused_computation.16 | convolution fusion | flops 6713245696 | bytes 16785408 | tf_op jit(solution)/shard_map/htc,hcv->thv/dot_general | solution.py:477
  150.1 1.4 copy.36
  151.5 1.0 reshape.32.ho_ref
  152.5 120.2 %back.1 = bf16[32,3584]{1,0:T(8,128)(2,1)} custom-call(bf16[4,4,32,512]{3,2,1,0:T(8,128)(2,1)} %reshape.32.ho_ref, bf16[512,3584]{1,0:T(8,128)(2,1)} %copy.39.wo_ref, bf16[32,3584]{1,0:T(8,128)(2,1)} %resid_ref.1, f32[1,3584]{1,0:T(1,128)} %broadcast_in_dim.30.gain_ref, f32[32,128]{1,0:T(8,128)} %select_maximum_fusion.meta_ref, bf16[3584,2048]{1,0:T(8,128)(2,1)} %bitcast.37, ...), custom_call_target="tpu_custom_call" | custom-call | tf_op jit(solution)/shard_map/back/pallas_call | solution.py:384
  272.7 1.6 copy.45
  (1 shorter events, 0.0 us)
Async XLA Ops:
  6.5 36.3 %all-gather.5.cloned.1.call-start = ((), (), s32[]{:S(2)}) async-start(), calls=%async_computation.1 | async-start | bytes 4128768 | tf_op jit(solution)/shard_map/all_gather | solution.py:479
  7.3 87.4 %all-gather.3.cloned.1.call-start = ((), (), s32[]{:S(2)}) async-start(), calls=%async_computation | async-start | bytes 4177920 | tf_op jit(solution)/shard_map/all_gather | solution.py:458
  94.6 15.7 %copy-start = (pred[512,3072]{0,1:T(8,128)(4,1)S(1)}, pred[512,3072]{0,1:T(8,128)(4,1)}, u32[]{:S(2)}) copy-start(pred[512,3072]{0,1:T(8,128)(4,1)} %iota_compare_fusion) | copy-start | bytes 4718596
Sparse Core Ops, SparseCore 0:
  9.0 33.7 all-gather.4
  45.0 49.5 all-gather.2

commit v2 on v1

--- a/solution.py
+++ b/solution.py
@@ -8,6 +8,7 @@
 from jax.sharding import PartitionSpec as P
 
 MESH = pl.DeviceIdType.MESH
+LOG2_E = 1.4426950408889634
 BF16, F32, I32 = jnp.bfloat16, jnp.float32, jnp.int32
 NEAR = (
     (1, 0), (0, 1), (3, 0), (0, 3), (1, 1), (3, 3), (1, 3), (3, 1),
@@ -118,8 +119,9 @@
 
     def project(h, k):
         head = ho_ref[k] if h == 0 else ho_ref[:, k]
-        value = dot(head.reshape(128, 512), wo_ref[:, half_cols(h)])
-        group(h, k, 0, 1792)[...] = value.astype(BF16).reshape(4, 32, 1792)
+        for b in range(2):
+            value = dot(head.reshape(128, 512), wo_ref[2 * h + b])
+            group(h, k, b * 896, 896)[...] = value.astype(BF16).reshape(4, 32, 896)
 
     def neighbour(h, phase, n):
         along_x = (h == 0) == (phase == 0)
@@ -434,6 +436,204 @@
     )(head_out, out_proj, resid, norm_gain, meta, expert_in, expert_down)
 
 
+LOWEST = -1e30
+
+
+def front_kernel(
+    scale, off_ref, q_ref, cache_ref, vup_ref, wo_ref,
+    ho_ref, wide_ref,
+    keys, kc, vt, qt, vupt, bias, acc, top, tot, pair,
+    k_s, k_r, w_s, w_r, own_sem,
+):
+    me = Place()
+    here = me.z * 2 + me.c
+
+    def along(axis, n):
+        if axis == 0:
+            return (here, up(me.x, n) * 4 + me.y)
+        return (here, me.x * 4 + up(me.y, n))
+
+    own_copy = pltpu.make_async_copy(cache_ref, keys.at[me.x, me.y], own_sem)
+    own_copy.start()
+
+    twin = (me.z * 2 + 1 - me.c, me.x * 4 + me.y)
+    above = [(up(me.z, n) * 2 + me.c, me.x * 4 + me.y) for n in (1, 3, 2)]
+    others = [along(0, 1), along(0, 3), along(1, 1), along(1, 3), twin] + above
+    barrier = pltpu.get_barrier_semaphore()
+    for other in others:
+        pl.semaphore_signal(barrier, inc=1, device_id=other, device_id_type=MESH)
+    pl.semaphore_wait(barrier, len(others))
+
+    def send(src, dst, ssem, rsem, device):
+        copy = pltpu.make_async_remote_copy(
+            src_ref=src, dst_ref=dst, send_sem=ssem, recv_sem=rsem,
+            device_id=device, device_id_type=MESH,
+        )
+        copy.start()
+        return copy
+
+    def axis_of(half, phase):
+        return half if phase == 0 else 1 - half
+
+    def spot(half, phase, n, lo, rows):
+        rows = pl.ds(half * 96 + lo, rows)
+        if axis_of(half, phase) == 0:
+            a = up(me.x, n)
+            return keys.at[a, me.y, rows] if phase == 0 else keys.at[a, :, rows]
+        b = up(me.y, n)
+        return keys.at[me.x, b, rows] if phase == 0 else keys.at[:, b, rows]
+
+    def sem(half, phase, k):
+        return (half * 2 + phase) * 4 + k
+
+    def spread(half, phase):
+        axis = axis_of(half, phase)
+        for k, n in ((0, 1), (1, 3)):
+            at = spot(half, phase, 0, 0, 96)
+            src = cache_ref.at[pl.ds(half * 96, 96)] if phase == 0 else at
+            i = sem(half, phase, k)
+            send(src, at, k_s.at[i], k_r.at[i], along(axis, n))
+
+    def forward(half, phase):
+        axis = axis_of(half, phase)
+        for k, n, lo in ((0, 3, 0), (1, 1, 48)):
+            whole(spot(half, phase, n, 0, 96), k_r.at[sem(half, phase, k)])
+            part = spot(half, phase, n, lo, 48)
+            i = sem(half, phase, 2 + k)
+            send(part, part, k_s.at[i], k_r.at[i], along(axis, 4 - n))
+
+    def far(half, phase):
+        for k, lo in ((0, 0), (1, 48)):
+            whole(spot(half, phase, 2, lo, 48), k_r.at[sem(half, phase, 2 + k)])
+
+    for half in range(2):
+        spread(half, 0)
+    send(wo_ref, pair, w_s.at[0], w_r.at[0], twin)
+
+    qt[:, pl.ds(576, 64), :] = jnp.zeros((4, 64, 512), BF16)
+    for h in range(2):
+        lo = h * 1152
+        qt[2 * h, pl.ds(0, 576), :] = q_ref[:, lo : lo + 640].T[:576]
+        qt[2 * h + 1, pl.ds(0, 576), :] = q_ref[:, lo + 512 : lo + 1152].T[64:]
+    for half in range(2):
+        forward(half, 0)
+    for h in range(4):
+        vupt[h] = vup_ref[h].T
+    kc[:, pl.ds(512, 128)] = jnp.zeros((768, 128), BF16)
+    top[...] = jnp.full((4, 1, 512), -3e38, F32)
+    tot[...] = jnp.zeros((4, 1, 512), F32)
+    acc[...] = jnp.zeros((4, 512, 512), F32)
+    whole(pair, w_r.at[0])
+    first = wo_ref[...]
+    second = pair[...]
+    low = jnp.where(me.c == 0, first, second)
+    high = jnp.where(me.c == 0, second, first)
+    wide_ref[me.z] = jnp.concatenate([low, high], axis=1)
+    own_copy.wait()
+    for half in range(2):
+        far(half, 0)
+    for half in range(2):
+        spread(half, 1)
+    rows = pl.ds(pl.multiple_of(me.c * 256, 256), 256)
+    for k, to in enumerate(above):
+        send(wide_ref.at[me.z, rows], wide_ref.at[me.z, rows], w_s.at[1 + k], w_r.at[1 + k], to)
+
+    row = lax.broadcasted_iota(I32, (768, 1), 0)
+    in_first = row < 384
+    low_row = jnp.where(in_first, row, row - 384)
+    nth = (low_row >= 96).astype(I32) + (low_row >= 192).astype(I32) + (low_row >= 288).astype(I32)
+    low_row = low_row - nth * 96
+    base = jnp.where(in_first, nth * 768 + low_row, nth * 192 + 96 + low_row)
+    query = lax.broadcasted_iota(I32, (768, 512), 1)
+
+    def step(i, carry):
+        @pl.when(i == 1)
+        def _():
+            for half in range(2):
+                forward(half, 1)
+
+        @pl.when(i == 3)
+        def _():
+            for half in range(2):
+                far(half, 1)
+            for k, n in enumerate((3, 1, 2)):
+                z = up(me.z, n)
+                got = wide_ref.at[z, rows]
+                whole(got, w_r.at[1 + k])
+                send(got, got, w_s.at[4 + k], w_r.at[4 + k], twin)
+
+        turn = i + lax.div(i, 2) - 2 * lax.div(i, 3)
+        b, a = up(me.y, turn), up(me.x, turn)
+        kc[pl.ds(0, 384), pl.ds(0, 576)] = keys[:, b, pl.ds(0, 96), :].reshape(384, 576)
+        kc[pl.ds(384, 384), pl.ds(0, 576)] = keys[a, :, pl.ds(96, 96), :].reshape(384, 576)
+        vt[...] = kc[:, pl.ds(0, 512)].T
+        start = jnp.where(in_first, b * 192, a * 768)
+        bias[...] = jnp.where(base + start - off_ref[0] <= query, 0.0, LOWEST)
+        for h in range(4):
+            s = dot(kc[...], qt[h]) * scale + bias[...]
+            old = top[h]
+            new = jnp.maximum(old, jnp.max(s, axis=0, keepdims=True))
+            p = jnp.exp2(s - new)
+            shrink = jnp.exp2(old - new)
+            top[h] = new
+            tot[h] = tot[h] * shrink + jnp.sum(p, axis=0, keepdims=True)
+            acc[h] = acc[h] * shrink + dot(vt[...], p.astype(BF16))
+        return carry
+
+    lax.fori_loop(0, 4, step, 0)
+    for h in range(4):
+        context = (acc[h] / tot[h]).astype(BF16)
+        value = dot(vupt[h], context).T.astype(BF16)
+        ho_ref[:, :, :, pl.ds(h * 128, 128)] = value.reshape(4, 4, 32, 128)
+    rest = pl.ds(pl.multiple_of(256 - me.c * 256, 256), 256)
+    for k, n in enumerate((3, 1, 2)):
+        z = up(me.z, n)
+        whole(wide_ref.at[z, rest], w_r.at[4 + k])
+        whole(wide_ref.at[z, rows], w_s.at[4 + k])
+        whole(wide_ref.at[me.z, rows], w_s.at[1 + k])
+    whole(wo_ref, w_s.at[0])
+    for half in range(2):
+        for phase in range(2):
+            for k in range(2):
+                whole(spot(half, phase, 0, 0, 96), k_s.at[sem(half, phase, k)])
+                whole(spot(half, phase, 0, 0, 48), k_s.at[sem(half, phase, 2 + k)])
+
+
+def front(offsets, queries, cache, value_up, out_proj, scale):
+    vmem = pl.BlockSpec(memory_space=pltpu.VMEM)
+    dma = pltpu.SemaphoreType.DMA
+    return pl.pallas_call(
+        functools.partial(front_kernel, scale),
+        out_shape=(
+            jax.ShapeDtypeStruct((4, 4, 32, 512), BF16),
+            jax.ShapeDtypeStruct((4, 512, 896), BF16),
+        ),
+        in_specs=[pl.BlockSpec(memory_space=pltpu.SMEM), vmem, vmem, vmem, vmem],
+        out_specs=(vmem, vmem),
+        scratch_shapes=[
+            pltpu.VMEM((4, 4, 192, 576), BF16),
+            pltpu.VMEM((768, 640), BF16),
+            pltpu.VMEM((512, 768), BF16),
+            pltpu.VMEM((4, 640, 512), BF16),
+            pltpu.VMEM((4, 128, 512), BF16),
+            pltpu.VMEM((768, 512), F32),
+            pltpu.VMEM((4, 512, 512), F32),
+            pltpu.VMEM((4, 1, 512), F32),
+            pltpu.VMEM((4, 1, 512), F32),
+            pltpu.VMEM((512, 448), BF16),
+            dma((16,)),
+            dma((16,)),
+            dma((7,)),
+            dma((7,)),
+            dma(()),
+        ],
+        compiler_params=pltpu.CompilerParams(
+            collective_id=2, has_side_effects=True, vmem_limit_bytes=60 * 1024 * 1024
+        ),
+        name="front",
+    )(offsets, queries, cache, value_up, out_proj)
+
+
 def shards(
     queries,
     cache,
@@ -447,36 +647,12 @@
     expert_in,
     expert_down,
 ):
-    heads_dev = value_up.shape[0]
     latent_width = value_up.shape[1]
     key_width = cache.shape[2]
-    tok_grp = queries.shape[0]
     score_scale = (value_up.shape[2] + key_width - latent_width) ** (-0.5)
-    query_heads = queries.reshape(tok_grp, heads_dev, key_width)
-    start_pos = offsets[0]
-    query_pos = start_pos + jnp.arange(tok_grp, dtype=jnp.int32)
-    key_rows = lax.all_gather(cache, "tensor", axis=1, tiled=True)[0]
-    key_count = key_rows.shape[0]
-    scores = (
-        jnp.einsum("thc,kc->htk", query_heads, key_rows, preferred_element_type=jnp.float32)
-        * score_scale
+    head_out, wide = front(
+        offsets, queries, cache[0], value_up, out_proj, score_scale * LOG2_E
     )
-    key_pos = jnp.arange(key_count, dtype=jnp.int32)
-    visible = key_pos[None, :] <= query_pos[:, None]
-    scores = jnp.where(visible[None], scores, jnp.float32(-1e30))
-    highest = jnp.max(scores, axis=2)
-    weights = jnp.where(visible[None], jnp.exp(scores - highest[..., None]), jnp.float32(0.0))
-    totals = jnp.sum(weights, axis=2)
-    weighted = jnp.einsum(
-        "htk,kc->htc",
-        weights.astype(jnp.bfloat16),
-        key_rows[:, :latent_width],
-        preferred_element_type=jnp.float32,
-    )
-    context = (weighted / totals[..., None]).astype(jnp.bfloat16)
-    head_out = jnp.einsum("htc,hcv->thv", context, value_up, preferred_element_type=jnp.float32)
-    head_out = head_out.astype(jnp.bfloat16).reshape(4, 4, 32, -1)
-    wide = lax.all_gather(out_proj, "dp", axis=1, tiled=True)
     meta = jnp.concatenate([routes.astype(F32), route_weights], axis=1)
     meta = jnp.pad(meta, ((0, 0), (0, 112)))
     return back(head_out, wide, resid, norm_gain[None], meta, expert_in[0], expert_down[0])

time: 282 us -> 180 us (0.64)
  waiting for transfers between devices: 72.6 us -> 0 us
  Pallas kernels: 120 us -> 172 us
  matrix products: 27 us -> 0 us
  other arithmetic: 27.8 us -> 1.37 us
  local copies, waits for them, and re-layouts: 19.5 us -> 5.82 us
  between operations: 14.1 us -> 0.67 us
    all_gather x2 -> x0, waiting for transfers between devices: 71.2 us -> none  [the longest x1 45.9 us: shards(): key_rows = lax.all_gather(cache, 'tensor', axis=1, tiled=True)[0]]
    pallas_call x0 -> x1, Pallas kernels: none -> 47.1 us  [front(): pl.pallas_call(functools.partial(front_kernel, scale), out_shape=(jax.Sha...]
    dot_general x2 -> x0, matrix products: 27 us -> none  [the longest x1 15.7 us: shards(): jnp.einsum('thc,kc->htk', query_heads, key_rows, preferred_element_type=j...]
    sub x1 -> x0, other arithmetic: 23.9 us -> none  [shards(): scores - highest[..., None]]
    all_gather x2 -> x0, local copies, waits for them, and re-layouts: 10.4 us -> none  [the longest x1 5.92 us: shards(): wide = lax.all_gather(out_proj, 'dp', axis=1, tiled=True)]
    pallas_call x1, Pallas kernels: 120 us -> 125 us  [back(): pl.pallas_call(back_kernel, out_shape=jax.ShapeDtypeStruct((32, 3584), BF...]
  transfers between devices with their start and end apart: 2 -> 0, of which waited for: 2 -> 0; matrix products, arithmetic and copies ran while one was open for 5% -> 0% of each run, Pallas kernels for 0% -> 0%
where the time goes in v2:
time: 180 us
  Pallas kernels  172 us (96%)
  local copies, waits for them, and re-layouts  5.82 us (3%)
    pallas_call x1, Pallas kernels, back(): pl.pallas_call(back_kernel, out_shape=jax.ShapeDtypeStruct((32, 3584), BF...  125 us
    pallas_call x1, Pallas kernels, front(): pl.pallas_call(functools.partial(front_kernel, scale), out_shape=(jax.Sha...  47.1 us
    unnamed x3, local copies, waits for them, and re-layouts  4.42 us

profile of v2, /device:TPU:1, one launch (start us, length us, event | category | flops | bytes accessed | tf_op | source)
XLA Modules:
  0.0 179.7 jit_solution(5170840204355412808)
XLA Ops:
  0.0 2.0 %copy.15.wo_ref = bf16[512,448]{1,0:T(8,128)(2,1)} copy(bf16[512,448]{0,1:T(8,128)(2,1)} %param.15) | data formatting | bytes 917504 | tf_op args[4]
  2.7 47.1 %front.1 = (bf16[4,4,32,512]{3,2,1,0:T(8,128)(2,1)}, bf16[4,512,896]{2,1,0:T(8,128)(2,1)}) custom-call(s32[1]{0:T(128)S(6)} %copy.19.off_ref, bf16[512,2304]{1,0:T(8,128)(2,1)} %q_ref.1, bf16[192,576]{1,0:T(8,128)(2,1)} %bitcast.5, bf16[4,512,128]{2,1,0:T(8,128)(2,1)} %vup_ref.1, bf16[512,448]{1,0:T(8,128)(2,1)} %copy.15.wo_ref), custom_call_target="tpu_custom_call" | custom-call | tf_op jit(solution)/shard_map/front/pallas_call | solution.py:605
  49.7 0.7 convert_element_type.5
  50.4 0.1 copy.16
  50.5 0.8 copy.17
  51.3 0.7 select_maximum_fusion.meta_ref
  52.0 1.3 broadcast_in_dim.3.gain_ref
  53.3 124.7 %back.1 = bf16[32,3584]{1,0:T(8,128)(2,1)} custom-call(bf16[4,4,32,512]{3,2,1,0:T(8,128)(2,1)} %get-tuple-element.7.ho_ref, bf16[4,512,896]{2,1,0:T(8,128)(2,1)} %get-tuple-element.8.wo_ref, bf16[32,3584]{1,0:T(8,128)(2,1)} %resid_ref.1, f32[1,3584]{1,0:T(1,128)} %broadcast_in_dim.3.gain_ref, f32[32,128]{1,0:T(8,128)} %select_maximum_fusion.meta_ref, ...), custom_call_target="tpu_custom_call" | custom-call | tf_op jit(solution)/shard_map/back/pallas_call | solution.py:386
  178.0 1.6 copy.20

commit v3 on v2

--- a/solution.py
+++ b/solution.py
@@ -14,10 +14,7 @@
     (1, 0), (0, 1), (3, 0), (0, 3), (1, 1), (3, 3), (1, 3), (3, 1),
     (2, 0), (0, 2), (2, 2), (2, 1), (1, 2), (2, 3), (3, 2),
 )
-ROUNDS = (
-    ((0, 0, 640), (1, 640, 640), (2, 1280, 512)),
-    ((0, 1792, 640), (1, 2432, 512), (2, 2944, 640)),
-)
+PARTS = ((0, 0, 1280), (1, 1280, 1152), (2, 2432, 1152))
 
 
 def whole(ref, sem):
@@ -81,17 +78,18 @@
 
 
 def back_kernel(
-    ho_ref, wo_ref, resid_ref, gain_ref, meta_ref, win_hbm, wdown_hbm,
+    ho_hbm, wo_hbm, resid_ref, gain_ref, routes_ref, weights_ref, win_hbm, wdown_hbm,
     out_ref,
-    win, wdown, part4, r1, l1, r2, l2, mid, r1b, l1b, r2b, l2b,
-    metas, pick, wgt, swap, stream, nrm, toks, outg, rows, stage, acc, hid, psum, recv,
+    ho_ref, wo_ref, win, wdown, part4, r1, l1, r2, l2, mid, r1b, l1b, r2b, l2b,
+    turned, table_ref, metas, pick, wgt, swap, stream, nrm, toks, outg, rows, stage, hid, half_sum, psum, recv,
     wsem, rs_s, rs_r, m_s, m_r, g_s, g_r, d_s, d_r, t_s, t_r, c_s, c_r,
 ):
     me = Place()
     loads = [
-        pltpu.make_async_copy(win_hbm.at[pl.ds(0, 1792)], win.at[pl.ds(0, 1792)], wsem.at[0]),
-        pltpu.make_async_copy(win_hbm.at[pl.ds(1792, 1792)], win.at[pl.ds(1792, 1792)], wsem.at[1]),
-        pltpu.make_async_copy(wdown_hbm, wdown, wsem.at[2]),
+        pltpu.make_async_copy(ho_hbm, ho_ref, wsem.at[0]),
+        pltpu.make_async_copy(wo_hbm, wo_ref, wsem.at[1]),
+        pltpu.make_async_copy(win_hbm, win, wsem.at[2]),
+        pltpu.make_async_copy(wdown_hbm, wdown, wsem.at[3]),
     ]
     for load in loads:
         load.start()
@@ -100,6 +98,10 @@
     others = partners(me)
     for other in others:
         pl.semaphore_signal(barrier, inc=1, device_id=other, device_id_type=MESH)
+    turned[...] = jnp.zeros((128, 128), F32)
+    turned[pl.ds(0, 8), pl.ds(0, 32)] = routes_ref[...].astype(F32)
+    turned[pl.ds(8, 8), pl.ds(0, 32)] = weights_ref[...]
+    table_ref[...] = turned[...].T[:32]
     pl.semaphore_wait(barrier, len(others))
 
     def send(src, dst, ssem, rsem, device):
@@ -191,9 +193,11 @@
                 if (n, core) == (0, 0):
                     continue
                 to = me.line(part, up(me.own_line(part), n), lax.rem(me.c + core, 2))
-                meta_sends.append(send(meta_ref, metas.at[part, own], m_s.at[part], m_r.at[part], to))
-        pltpu.make_async_copy(meta_ref, metas.at[part, own], m_r.at[part]).start()
-
+                meta_sends.append(send(table_ref, metas.at[part, own], m_s.at[part], m_r.at[part], to))
+        pltpu.make_async_copy(table_ref, metas.at[part, own], m_r.at[part]).start()
+
+    loads[0].wait()
+    loads[1].wait()
     for h in range(2):
         project(h, up(position(h, 0), 2))
     for h in range(2):
@@ -209,11 +213,10 @@
     token = lax.broadcasted_iota(I32, (256, 256), 0)
     other = lax.broadcasted_iota(I32, (256, 256), 1)
     earlier = jnp.where((token // 32 == other // 32) & (other < token), 1.0, 0.0).astype(BF16)
-    lane = lax.broadcasted_iota(I32, (128, 512), 1)
-    spread = jnp.where(lane // 32 == lax.broadcasted_iota(I32, (128, 512), 0), 1.0, 0.0).astype(BF16)
-    slot = lax.broadcasted_iota(I32, (256, 512), 1) % 32
-    of_source = slot // 4 == lax.broadcasted_iota(I32, (256, 512), 0) // 32
-    rank_wanted = (slot % 4).astype(F32)
+    lane = lax.broadcasted_iota(I32, (128, 256), 1)
+    spread = jnp.where(lane // 16 == lax.broadcasted_iota(I32, (128, 256), 0), 1.0, 0.0).astype(BF16)
+    of_source = other % 16 // 2 == token // 32
+    rank_wanted = (other % 2).astype(F32)
     for part in range(3):
         whole(metas.at[part], m_r.at[part])
         table = metas[part].reshape(256, 128)
@@ -227,14 +230,15 @@
             weight = jnp.where(same, table[:, 8 + k : 9 + k], weight)
         rank = dot(earlier, hit.astype(BF16))
         rank = jnp.where(hit > 0.5, rank, -1.0)
-        chosen = (dot(rank.astype(BF16), spread) == rank_wanted) & of_source
-        pick[part] = jnp.where(chosen, 1.0, 0.0).T.astype(BF16)
-        wgt[part] = jnp.where(chosen, dot(weight.astype(BF16), spread), 0.0).astype(BF16)
-    row = lax.broadcasted_iota(I32, (512, 512), 0)
-    col = lax.broadcasted_iota(I32, (512, 512), 1)
-    rx, ry, rz, low = row // 128, (row // 32) % 4, (row // 8) % 4, row % 8
-    swap[0] = jnp.where(col == rz * 128 + ry * 32 + rx * 8 + low, 1.0, 0.0).astype(BF16)
-    swap[1] = jnp.where(col == rx * 128 + rz * 32 + ry * 8 + low, 1.0, 0.0).astype(BF16)
+        rank = jnp.where(of_source, dot(rank.astype(BF16), spread) - rank_wanted, -1.0)
+        weight = dot(weight.astype(BF16), spread)
+        for half in range(2):
+            chosen = rank == half * 2.0
+            pick[part, half] = jnp.where(chosen, 1.0, 0.0).T.astype(BF16)
+            wgt[part, half] = jnp.where(chosen, weight, 0.0).astype(BF16)
+    rx, ry, rz, low = token // 64, token // 16 % 4, token // 4 % 4, token % 4
+    swap[0] = jnp.where(other == rz * 64 + ry * 16 + rx * 4 + low, 1.0, 0.0).astype(BF16)
+    swap[1] = jnp.where(other == rx * 64 + rz * 16 + ry * 4 + low, 1.0, 0.0).astype(BF16)
 
     for h in range(2):
         second(h, 0)
@@ -250,148 +254,144 @@
         stream[:, half_cols(h)] = last(h, 1) + resid_ref[:, half_cols(h)].astype(F32)
     value = stream[...]
     mean_square = jnp.mean(value * value, axis=1, keepdims=True)
-    nrm[...] = (value * lax.rsqrt(mean_square + 1e-06) * gain_ref[...]).astype(BF16)
+    nrm[...] = (value * lax.rsqrt(mean_square + 1e-06) * gain_ref[...].reshape(1, 3584)).astype(BF16)
     for copy in started.values():
         copy.wait_send()
 
-    def gather(i):
-        for p, (part, lo, n) in enumerate(ROUNDS[i]):
-            own = me.own_line(part) * 2 + me.c
-            at = i * 3 + p
-            for step, core in ((0, 1), (1, 0), (3, 0), (1, 1), (3, 1), (2, 0), (2, 1)):
-                to = me.line(part, up(me.own_line(part), step), lax.rem(me.c + core, 2))
-                send(nrm.at[:, pl.ds(lo, n)], toks.at[own, :, pl.ds(lo, n)], g_s.at[at], g_r.at[at], to)
-            pltpu.make_async_copy(nrm.at[:, pl.ds(lo, n)], toks.at[own, :, pl.ds(lo, n)], g_r.at[at]).start()
-
-    def flat(ref, lo, n):
-        return ref[:, :, :, pl.ds(lo, n)].reshape(512, n)
-
-    def exchange(i, src, dst_of, ssem, rsem):
+    LINE = ((0, 1), (1, 0), (3, 0), (1, 1), (3, 1), (2, 0), (2, 1))
+    for part, lo, n in PARTS:
+        cols = pl.ds(lo, n)
+        own = me.own_line(part) * 2 + me.c
+        for step, core in LINE:
+            to = me.line(part, up(me.own_line(part), step), lax.rem(me.c + core, 2))
+            send(nrm.at[:, cols], toks.at[own, :, cols], g_s.at[part], g_r.at[part], to)
+        pltpu.make_async_copy(nrm.at[:, cols], toks.at[own, :, cols], g_r.at[part]).start()
+
+    def half_of(ref, half):
+        if ref is part4:
+            return lambda b1, b2, cols: part4.at[b1, b2, pl.ds(half * 16, 16), cols]
+        return lambda b1, b2, cols: ref.at[half, b1, b2, :, cols]
+
+    def exchange(half, src, dst_of, ssem, rsem, parts):
         for d1, d2 in NEAR:
-            for p, (part, lo, n) in enumerate(ROUNDS[i]):
+            for part, lo, n in parts:
                 b1, b2 = me.own_plane(part)
                 e1, e2 = up(b1, d1), up(b2, d2)
+                at, cols = half * 3 + part, pl.ds(lo, n)
                 send(
-                    src.at[e1, e2, :, pl.ds(lo, n)], dst_of(part).at[b1, b2, :, pl.ds(lo, n)],
-                    ssem.at[i * 3 + p], rsem.at[i * 3 + p], me.plane(part, e1, e2),
+                    half_of(src, half)(e1, e2, cols), half_of(dst_of(part), half)(b1, b2, cols),
+                    ssem.at[at], rsem.at[at], me.plane(part, e1, e2),
                 )
-        for p, (part, lo, n) in enumerate(ROUNDS[i]):
+        for part, lo, n in parts:
             b1, b2 = me.own_plane(part)
+            at, cols = half * 3 + part, pl.ds(lo, n)
             pltpu.make_async_copy(
-                src.at[b1, b2, :, pl.ds(lo, n)], dst_of(part).at[b1, b2, :, pl.ds(lo, n)],
-                rsem.at[i * 3 + p],
+                half_of(src, half)(b1, b2, cols), half_of(dst_of(part), half)(b1, b2, cols), rsem.at[at]
             ).start()
 
     def landing(part):
         return rows if part == 0 else stage
 
-    def block(ref, lo, n):
-        return ref.at[:, :, :, pl.ds(lo, n)]
-
-    def sent(ref, lo, n, sem):
+    def sent(half, lo, n, sem):
         for k in range(3):
-            whole(ref.at[k, :, :, pl.ds(lo, n)], sem)
-        whole(ref.at[3, pl.ds(0, 3), :, pl.ds(lo, n)], sem)
-
-    def dispatch(i):
-        for p, (part, lo, n) in enumerate(ROUNDS[i]):
-            whole(toks.at[:, :, pl.ds(lo, n)], g_r.at[i * 3 + p])
-            value = dot(pick[part], toks[:, :, pl.ds(lo, n)].reshape(256, n))
-            outg[:, :, :, pl.ds(lo, n)] = value.astype(BF16).reshape(4, 4, 32, n)
-        exchange(i, outg, landing, d_s, d_r)
-
-    def arrive(i):
-        for p, (part, lo, n) in enumerate(ROUNDS[i]):
-            whole(block(landing(part), lo, n), d_r.at[i * 3 + p])
+            whole(outg.at[half, k, :, :, pl.ds(lo, n)], sem)
+        whole(outg.at[half, 3, pl.ds(0, 3), :, pl.ds(lo, n)], sem)
+
+    def dispatch(half):
+        for part, lo, n in PARTS:
+            cols = pl.ds(lo, n)
+            if half == 0:
+                whole(toks.at[:, :, cols], g_r.at[part])
+            value = dot(pick[part, half], toks[:, :, cols].reshape(256, n))
+            outg[half, :, :, :, cols] = value.astype(BF16).reshape(4, 4, 16, n)
+        exchange(half, outg, landing, d_s, d_r, PARTS)
+
+    def expert(half):
+        for part, lo, n in PARTS:
+            cols = pl.ds(lo, n)
+            whole(landing(part).at[half, :, :, :, cols], d_r.at[half * 3 + part])
             if part:
-                value = dot(swap[part - 1], flat(stage, lo, n))
-                rows[:, :, :, pl.ds(lo, n)] = value.astype(BF16).reshape(4, 4, 32, n)
-
-    gather(0)
-    gather(1)
+                value = dot(swap[part - 1], stage[half, :, :, :, cols].reshape(256, n))
+                rows[half, :, :, :, cols] = value.astype(BF16).reshape(4, 4, 16, n)
+        if half == 0:
+            loads[2].wait()
+            loads[3].wait()
+
+        def hidden(j, carry):
+            cols = pl.ds(pl.multiple_of(j * 256, 256), 256)
+            more = pl.ds(pl.multiple_of(j * 256 + 1024, 256), 256)
+            here = rows[half].reshape(256, 3584)
+            gate = dot(here, win[:, cols])
+            lift = dot(here, win[:, more])
+            hid[0, :, cols] = (gate / (1.0 + jnp.exp(-gate)) * lift).astype(BF16)
+            return carry
+
+        lax.fori_loop(0, 4, hidden, 0)
+        for part, lo, n in PARTS:
+            if part:
+                hid[part] = dot(swap[part - 1], hid[0]).astype(BF16)
+            sent(half, lo, n, d_s.at[half * 3 + part])
+            value = dot(hid[part], wdown[:, pl.ds(lo, n)])
+            outg[half, :, :, :, pl.ds(lo, n)] = value.astype(BF16).reshape(4, 4, 16, n)
+            if half:
+                exchange(half, outg, lambda part: part4, t_s, t_r, ((part, lo, n),))
+        if half == 0:
+            exchange(half, outg, lambda part: part4, t_s, t_r, PARTS)
+
     dispatch(0)
     dispatch(1)
-
-    loads[0].wait()
-    arrive(0)
-
-    def first_half(j, carry):
-        cols = pl.ds(pl.multiple_of(j * 256, 256), 256)
-        acc[:, cols] = dot(flat(rows, 0, 1792), win[pl.ds(0, 1792), cols])
-        return carry
-
-    lax.fori_loop(0, 8, first_half, 0)
-    loads[1].wait()
-    arrive(1)
-
-    def second_half(j, carry):
-        cols = pl.ds(pl.multiple_of(j * 256, 256), 256)
-        more = pl.ds(pl.multiple_of(j * 256 + 1024, 256), 256)
-        gate = acc[:, cols] + dot(flat(rows, 1792, 1792), win[pl.ds(1792, 1792), cols])
-        lift = acc[:, more] + dot(flat(rows, 1792, 1792), win[pl.ds(1792, 1792), more])
-        hid[0, :, cols] = (gate / (1.0 + jnp.exp(-gate)) * lift).astype(BF16)
-        return carry
-
-    lax.fori_loop(0, 4, second_half, 0)
-    loads[2].wait()
-    for part in (1, 2):
-        hid[part] = dot(swap[part - 1], hid[0]).astype(BF16)
-    for i in range(2):
-        for p, (part, lo, n) in enumerate(ROUNDS[i]):
-            sent(outg, lo, n, d_s.at[i * 3 + p])
-            whole_gather = toks.at[pl.ds(0, 7), :, pl.ds(lo, n)]
-            whole(whole_gather, g_s.at[i * 3 + p])
-            value = dot(hid[part], wdown[:, pl.ds(lo, n)])
-            outg[:, :, :, pl.ds(lo, n)] = value.astype(BF16).reshape(4, 4, 32, n)
-        exchange(i, outg, lambda part: part4, t_s, t_r)
-
-    for i in range(2):
-        for p, (part, lo, n) in enumerate(ROUNDS[i]):
-            at = i * 3 + p
-            whole(block(part4, lo, n), t_r.at[at])
-            value = dot(wgt[part], flat(part4, lo, n))
-            psum[:, :, pl.ds(lo, n)] = value.astype(BF16).reshape(8, 32, n)
+    expert(0)
+    expert(1)
+
+    for half in range(2):
+        for part, lo, n in PARTS:
+            cols = pl.ds(lo, n)
+            back_rows = part4.at[:, :, pl.ds(half * 16, 16), cols]
+            whole(back_rows, t_r.at[half * 3 + part])
+            value = dot(wgt[part, half], back_rows[...].reshape(256, n))
+            if half == 0:
+                half_sum[:, cols] = value
+                continue
+            psum[:, :, cols] = (half_sum[:, cols] + value).astype(BF16).reshape(8, 32, n)
             own = me.own_line(part) * 2 + me.c
-            for step, core in ((0, 1), (1, 0), (3, 0), (1, 1), (3, 1), (2, 0), (2, 1)):
+            for step, core in LINE:
                 a, k = up(me.own_line(part), step), lax.rem(me.c + core, 2)
                 send(
-                    psum.at[a * 2 + k, :, pl.ds(lo, n)], recv.at[own, :, pl.ds(lo, n)],
-                    c_s.at[at], c_r.at[at], me.line(part, a, k),
+                    psum.at[a * 2 + k, :, cols], recv.at[own, :, cols],
+                    c_s.at[part], c_r.at[part], me.line(part, a, k),
                 )
-            pltpu.make_async_copy(
-                psum.at[own, :, pl.ds(lo, n)], recv.at[own, :, pl.ds(lo, n)], c_r.at[at]
-            ).start()
-    for i in range(2):
-        for p, (part, lo, n) in enumerate(ROUNDS[i]):
-            at = i * 3 + p
-            whole(recv.at[:, :, pl.ds(lo, n)], c_r.at[at])
-            total = stream[:, pl.ds(lo, n)]
-            for q in range(8):
-                total += recv[q, :, pl.ds(lo, n)].astype(F32)
-            out_ref[:, pl.ds(lo, n)] = total.astype(BF16)
-    for i in range(2):
-        for p, (part, lo, n) in enumerate(ROUNDS[i]):
-            at = i * 3 + p
-            sent(outg, lo, n, t_s.at[at])
-            whole(psum.at[pl.ds(0, 7), :, pl.ds(lo, n)], c_s.at[at])
-    for part in range(3):
+            pltpu.make_async_copy(psum.at[own, :, cols], recv.at[own, :, cols], c_r.at[part]).start()
+    for part, lo, n in PARTS:
+        cols = pl.ds(lo, n)
+        whole(recv.at[:, :, cols], c_r.at[part])
+        total = stream[:, cols]
+        for q in range(8):
+            total += recv[q, :, cols].astype(F32)
+        out_ref[:, cols] = total.astype(BF16)
+    for part, lo, n in PARTS:
+        for half in range(2):
+            sent(half, lo, n, t_s.at[half * 3 + part])
+        whole(toks.at[pl.ds(0, 7), :, pl.ds(lo, n)], g_s.at[part])
+        whole(psum.at[pl.ds(0, 7), :, pl.ds(lo, n)], c_s.at[part])
         whole(metas.at[part, pl.ds(0, 7)], m_s.at[part])
 
 
-def back(head_out, out_proj, resid, norm_gain, meta, expert_in, expert_down):
+def back(head_out, out_proj, resid, norm_gain, routes, weights, expert_in, expert_down):
     vmem = pl.BlockSpec(memory_space=pltpu.VMEM)
     hbm = pl.BlockSpec(memory_space=pl.ANY)
     dma = pltpu.SemaphoreType.DMA
-    grid_rows = (4, 4, 32, 3584)
+    halves = (2, 4, 4, 16, 3584)
     return pl.pallas_call(
         back_kernel,
         out_shape=jax.ShapeDtypeStruct((32, 3584), BF16),
-        in_specs=[vmem, vmem, vmem, vmem, vmem, hbm, hbm],
+        in_specs=[hbm, hbm, vmem, vmem, vmem, vmem, hbm, hbm],
         out_specs=vmem,
         scratch_shapes=[
+            pltpu.VMEM((4, 4, 32, 512), BF16),
+            pltpu.VMEM((4, 512, 896), BF16),
             pltpu.VMEM((3584, 2048), BF16),
             pltpu.VMEM((1024, 3584), BF16),
-            pltpu.VMEM(grid_rows, BF16),
+            pltpu.VMEM((4, 4, 32, 3584), BF16),
             pltpu.VMEM((2, 4, 32, 896), BF16),
             pltpu.VMEM((2, 4, 32, 896), BF16),
             pltpu.VMEM((2, 4, 32, 1792), BF16),
@@ -401,48 +401,50 @@
             pltpu.VMEM((2, 32, 896), BF16),
             pltpu.VMEM((2, 32, 1792), BF16),
             pltpu.VMEM((2, 32, 1792), BF16),
+            pltpu.VMEM((128, 128), F32),
+            pltpu.VMEM((32, 128), F32),
             pltpu.VMEM((3, 8, 32, 128), F32),
-            pltpu.VMEM((3, 512, 256), BF16),
-            pltpu.VMEM((3, 256, 512), BF16),
-            pltpu.VMEM((2, 512, 512), BF16),
+            pltpu.VMEM((3, 2, 256, 256), BF16),
+            pltpu.VMEM((3, 2, 256, 256), BF16),
+            pltpu.VMEM((2, 256, 256), BF16),
             pltpu.VMEM((32, 3584), F32),
             pltpu.VMEM((32, 3584), BF16),
             pltpu.VMEM((8, 32, 3584), BF16),
-            pltpu.VMEM(grid_rows, BF16),
-            pltpu.VMEM(grid_rows, BF16),
-            pltpu.VMEM(grid_rows, BF16),
-            pltpu.VMEM((512, 2048), F32),
-            pltpu.VMEM((3, 512, 1024), BF16),
+            pltpu.VMEM(halves, BF16),
+            pltpu.VMEM(halves, BF16),
+            pltpu.VMEM(halves, BF16),
+            pltpu.VMEM((3, 256, 1024), BF16),
+            pltpu.VMEM((256, 3584), F32),
             pltpu.VMEM((8, 32, 3584), BF16),
             pltpu.VMEM((8, 32, 3584), BF16),
-            dma((3,)),
+            dma((4,)),
             dma((24,)),
             dma((24,)),
+            dma((3,)),
+            dma((3,)),
             dma((3,)),
             dma((3,)),
             dma((6,)),
             dma((6,)),
             dma((6,)),
             dma((6,)),
-            dma((6,)),
-            dma((6,)),
-            dma((6,)),
-            dma((6,)),
+            dma((3,)),
+            dma((3,)),
         ],
         compiler_params=pltpu.CompilerParams(
             collective_id=1, has_side_effects=True, vmem_limit_bytes=67043328
         ),
         name="back",
-    )(head_out, out_proj, resid, norm_gain, meta, expert_in, expert_down)
+    )(head_out, out_proj, resid, norm_gain, routes, weights, expert_in, expert_down)
 
 
 LOWEST = -1e30
 
 
 def front_kernel(
-    scale, off_ref, q_ref, cache_ref, vup_ref, wo_ref,
+    scale, off_ref, q_ref, cache_ref, vup_ref, wot_ref,
     ho_ref, wide_ref,
-    keys, kc, vt, qt, vupt, bias, acc, top, tot, pair,
+    keys, kc, vt, qt, vupt, bias, scores, acc, top, tot, wo_ref, pair,
     k_s, k_r, w_s, w_r, own_sem,
 ):
     me = Place()
@@ -456,6 +458,7 @@
     own_copy = pltpu.make_async_copy(cache_ref, keys.at[me.x, me.y], own_sem)
     own_copy.start()
 
+    wo_ref[...] = wot_ref[...].T
     twin = (me.z * 2 + 1 - me.c, me.x * 4 + me.y)
     above = [(up(me.z, n) * 2 + me.c, me.x * 4 + me.y) for n in (1, 3, 2)]
     others = [along(0, 1), along(0, 3), along(1, 1), along(1, 3), twin] + above
@@ -566,11 +569,18 @@
         b, a = up(me.y, turn), up(me.x, turn)
         kc[pl.ds(0, 384), pl.ds(0, 576)] = keys[:, b, pl.ds(0, 96), :].reshape(384, 576)
         kc[pl.ds(384, 384), pl.ds(0, 576)] = keys[a, :, pl.ds(96, 96), :].reshape(384, 576)
+
+        def score(u):
+            scores[u % 2] = dot(kc[...], qt[u])
+
+        score(0)
         vt[...] = kc[:, pl.ds(0, 512)].T
         start = jnp.where(in_first, b * 192, a * 768)
         bias[...] = jnp.where(base + start - off_ref[0] <= query, 0.0, LOWEST)
         for h in range(4):
-            s = dot(kc[...], qt[h]) * scale + bias[...]
+            if h < 3:
+                score(h + 1)
+            s = scores[h % 2] * scale + bias[...]
             old = top[h]
             new = jnp.maximum(old, jnp.max(s, axis=0, keepdims=True))
             p = jnp.exp2(s - new)
@@ -617,9 +627,11 @@
             pltpu.VMEM((4, 640, 512), BF16),
             pltpu.VMEM((4, 128, 512), BF16),
             pltpu.VMEM((768, 512), F32),
+            pltpu.VMEM((2, 768, 512), F32),
             pltpu.VMEM((4, 512, 512), F32),
             pltpu.VMEM((4, 1, 512), F32),
             pltpu.VMEM((4, 1, 512), F32),
+            pltpu.VMEM((512, 448), BF16),
             pltpu.VMEM((512, 448), BF16),
             dma((16,)),
             dma((16,)),
@@ -651,11 +663,11 @@
     key_width = cache.shape[2]
     score_scale = (value_up.shape[2] + key_width - latent_width) ** (-0.5)
     head_out, wide = front(
-        offsets, queries, cache[0], value_up, out_proj, score_scale * LOG2_E
+        offsets, queries, cache[0], value_up, out_proj.T, score_scale * LOG2_E
     )
-    meta = jnp.concatenate([routes.astype(F32), route_weights], axis=1)
-    meta = jnp.pad(meta, ((0, 0), (0, 112)))
-    return back(head_out, wide, resid, norm_gain[None], meta, expert_in[0], expert_down[0])
+    return back(
+        head_out, wide, resid, norm_gain, routes.T, route_weights.T, expert_in[0], expert_down[0]
+    )
 
 
 def solution(mesh):

time: 180 us -> 162 us (0.900)
  Pallas kernels: 172 us -> 160 us
  local copies, waits for them, and re-layouts: 5.82 us -> 1.64 us
    pallas_call x1, Pallas kernels: 125 us -> 115 us  [back(): pl.pallas_call(back_kernel, out_shape=jax.ShapeDtypeStruct((32, 3584), BF...]
    unnamed x3 -> x1, local copies, waits for them, and re-layouts: 4.42 us -> 1.64 us
where the time goes in v3:
time: 162 us
  Pallas kernels  160 us (99%)
  local copies, waits for them, and re-layouts  1.64 us (1%)
    pallas_call x1, Pallas kernels, back(): pl.pallas_call(back_kernel, out_shape=jax.ShapeDtypeStruct((32, 3584), BF...  115 us
    pallas_call x1, Pallas kernels, front(): pl.pallas_call(functools.partial(front_kernel, scale), out_shape=(jax.Sha...  45.3 us

profile of v3, /device:TPU:1, one launch (start us, length us, event | category | flops | bytes accessed | tf_op | source)
XLA Modules:
  0.0 162.2 jit_solution(4614760980011526288)
XLA Ops:
  0.7 45.3 %front.1 = (bf16[4,4,32,512]{3,2,1,0:T(8,128)(2,1)}, bf16[4,512,896]{2,1,0:T(8,128)(2,1)}) custom-call(s32[1]{0:T(128)S(6)} %copy.13.off_ref, bf16[512,2304]{1,0:T(8,128)(2,1)} %q_ref.1, bf16[192,576]{1,0:T(8,128)(2,1)} %bitcast.9, bf16[4,512,128]{2,1,0:T(8,128)(2,1)} %vup_ref.1, bf16[448,512]{1,0:T(8,128)(2,1)} %bitcast.8), custom_call_target="tpu_custom_call" | custom-call | tf_op jit(solution)/shard_map/front/pallas_call | solution.py:615
  46.0 114.6 %back.1 = bf16[32,3584]{1,0:T(8,128)(2,1)} custom-call(bf16[4,4,32,512]{3,2,1,0:T(8,128)(2,1)} %get-tuple-element.7.ho_hbm, bf16[4,512,896]{2,1,0:T(8,128)(2,1)} %get-tuple-element.8.wo_hbm, bf16[32,3584]{1,0:T(8,128)(2,1)} %resid_ref.1, f32[3584]{0:T(1024)} %gain_ref.1, s32[8,32]{1,0:T(8,128)} %bitcast.10, f32[8,32]{1,0:T(8,128)} %bitcast.11, ...), custom_call_target="tpu_custom_call" | custom-call | tf_op jit(solution)/shard_map/back/pallas_call | solution.py:384
  160.6 1.6 %copy.14 = bf16[32,3584]{1,0:T(8,128)(2,1)} copy(bf16[32,3584]{1,0:T(8,128)(2,1)} %back.1) | data formatting | bytes 458752

commit v4 on v3

--- a/solution.py
+++ b/solution.py
@@ -78,30 +78,30 @@
 
 
 def back_kernel(
-    ho_hbm, wo_hbm, resid_ref, gain_ref, routes_ref, weights_ref, win_hbm, wdown_hbm,
+    stream_ref, gain_ref, routes_ref, weights_ref, win_hbm, wdown_hbm,
     out_ref,
-    ho_ref, wo_ref, win, wdown, part4, r1, l1, r2, l2, mid, r1b, l1b, r2b, l2b,
-    turned, table_ref, metas, pick, wgt, swap, stream, nrm, toks, outg, rows, stage, hid, half_sum, psum, recv,
-    wsem, rs_s, rs_r, m_s, m_r, g_s, g_r, d_s, d_r, t_s, t_r, c_s, c_r,
+    win, wdown, part4, turned, table_ref, metas, pick, wgt, swap,
+    nrm, toks, outg, rows, stage, hid, half_sum, psum, recv,
+    wsem, m_s, m_r, g_s, g_r, d_s, d_r, t_s, t_r, c_s, c_r,
 ):
     me = Place()
-    loads = [
-        pltpu.make_async_copy(ho_hbm, ho_ref, wsem.at[0]),
-        pltpu.make_async_copy(wo_hbm, wo_ref, wsem.at[1]),
-        pltpu.make_async_copy(win_hbm, win, wsem.at[2]),
-        pltpu.make_async_copy(wdown_hbm, wdown, wsem.at[3]),
-    ]
-    for load in loads:
-        load.start()
-
     barrier = pltpu.get_barrier_semaphore()
     others = partners(me)
     for other in others:
         pl.semaphore_signal(barrier, inc=1, device_id=other, device_id_type=MESH)
+    loads = [
+        pltpu.make_async_copy(win_hbm, win, wsem.at[0]),
+        pltpu.make_async_copy(wdown_hbm, wdown, wsem.at[1]),
+    ]
+    for load in loads:
+        load.start()
     turned[...] = jnp.zeros((128, 128), F32)
     turned[pl.ds(0, 8), pl.ds(0, 32)] = routes_ref[...].astype(F32)
     turned[pl.ds(8, 8), pl.ds(0, 32)] = weights_ref[...]
     table_ref[...] = turned[...].T[:32]
+    value = stream_ref[...]
+    mean_square = jnp.mean(value * value, axis=1, keepdims=True)
+    nrm[...] = (value * lax.rsqrt(mean_square + 1e-06) * gain_ref[...].reshape(1, 3584)).astype(BF16)
     pl.semaphore_wait(barrier, len(others))
 
     def send(src, dst, ssem, rsem, device):
@@ -111,79 +111,6 @@
         )
         copy.start()
         return copy
-
-    def half_cols(h):
-        return pl.ds(h * 1792, 1792)
-
-    def group(h, k, lo, n):
-        cols = pl.ds(h * 1792 + lo, n)
-        return part4.at[k, :, :, cols] if h == 0 else part4.at[:, k, :, cols]
-
-    def project(h, k):
-        head = ho_ref[k] if h == 0 else ho_ref[:, k]
-        for b in range(2):
-            value = dot(head.reshape(128, 512), wo_ref[2 * h + b])
-            group(h, k, b * 896, 896)[...] = value.astype(BF16).reshape(4, 32, 896)
-
-    def neighbour(h, phase, n):
-        along_x = (h == 0) == (phase == 0)
-        if along_x:
-            return (me.z * 2 + me.c, up(me.x, n) * 4 + me.y)
-        return (me.z * 2 + me.c, me.x * 4 + up(me.y, n))
-
-    def position(h, phase):
-        return me.x if (h == 0) == (phase == 0) else me.y
-
-    def piece(h, phase, k, lo, n):
-        return group(h, k, lo, n) if phase == 0 else mid.at[h, k, :, pl.ds(lo, n)]
-
-    def boxes(phase):
-        return (r1, l1, r2, l2) if phase == 0 else (r1b, l1b, r2b, l2b)
-
-    def box(ref, h, phase, lo, n):
-        if phase == 0:
-            return ref.at[h, :, :, pl.ds(lo, n)]
-        return ref.at[h, :, pl.ds(lo, n)]
-
-    started = {}
-
-    def first_far(h, phase):
-        k = up(position(h, phase), 2)
-        br1, bl1, _, _ = boxes(phase)
-        for side, (ref, lo, n) in enumerate(((br1, 0, 1), (bl1, 896, 3))):
-            i = (h * 2 + phase) * 6 + side
-            started[h, phase, side] = send(
-                piece(h, phase, k, lo, 896), box(ref, h, phase, 0, 896),
-                rs_s.at[i], rs_r.at[i], neighbour(h, phase, n),
-            )
-
-    def first_near(h, phase):
-        _, _, br2, bl2 = boxes(phase)
-        for side, (ref, lo, n) in enumerate(((br2, 896, 1), (bl2, 0, 3))):
-            i = (h * 2 + phase) * 6 + 2 + side
-            started[h, phase, 2 + side] = send(
-                piece(h, phase, up(position(h, phase), n), lo, 896), box(ref, h, phase, lo, 896),
-                rs_s.at[i], rs_r.at[i], neighbour(h, phase, n),
-            )
-
-    def second(h, phase):
-        br1, bl1, br2, bl2 = boxes(phase)
-        for side, (ref, to, lo, n) in enumerate(((br1, br2, 0, 1), (bl1, bl2, 896, 3))):
-            i = (h * 2 + phase) * 6 + 4 + side
-            started[h, phase, side].wait_recv()
-            mine = piece(h, phase, up(position(h, phase), n), lo, 896)
-            mine[...] = (mine[...].astype(F32) + box(ref, h, phase, 0, 896)[...].astype(F32)).astype(BF16)
-            started[h, phase, 4 + side] = send(
-                mine, box(to, h, phase, lo, 896), rs_s.at[i], rs_r.at[i], neighbour(h, phase, n)
-            )
-
-    def last(h, phase):
-        for i in (2, 3, 4, 5):
-            started[h, phase, i].wait_recv()
-        _, _, br2, bl2 = boxes(phase)
-        total = piece(h, phase, position(h, phase), 0, 1792)[...].astype(F32)
-        total += box(br2, h, phase, 0, 1792)[...].astype(F32)
-        return total + box(bl2, h, phase, 0, 1792)[...].astype(F32)
 
     meta_sends = []
     for part in range(3):
@@ -196,19 +123,14 @@
                 meta_sends.append(send(table_ref, metas.at[part, own], m_s.at[part], m_r.at[part], to))
         pltpu.make_async_copy(table_ref, metas.at[part, own], m_r.at[part]).start()
 
-    loads[0].wait()
-    loads[1].wait()
-    for h in range(2):
-        project(h, up(position(h, 0), 2))
-    for h in range(2):
-        first_far(h, 0)
-    for n in (1, 3):
-        for h in range(2):
-            project(h, up(position(h, 0), n))
-    for h in range(2):
-        first_near(h, 0)
-    for h in range(2):
-        project(h, position(h, 0))
+    LINE = ((0, 1), (1, 0), (3, 0), (1, 1), (3, 1), (2, 0), (2, 1))
+    for part, lo, n in PARTS:
+        cols = pl.ds(lo, n)
+        own = me.own_line(part) * 2 + me.c
+        for step, core in LINE:
+            to = me.line(part, up(me.own_line(part), step), lax.rem(me.c + core, 2))
+            send(nrm.at[:, cols], toks.at[own, :, cols], g_s.at[part], g_r.at[part], to)
+        pltpu.make_async_copy(nrm.at[:, cols], toks.at[own, :, cols], g_r.at[part]).start()
 
     token = lax.broadcasted_iota(I32, (256, 256), 0)
     other = lax.broadcasted_iota(I32, (256, 256), 1)
@@ -240,33 +162,6 @@
     swap[0] = jnp.where(other == rz * 64 + ry * 16 + rx * 4 + low, 1.0, 0.0).astype(BF16)
     swap[1] = jnp.where(other == rx * 64 + rz * 16 + ry * 4 + low, 1.0, 0.0).astype(BF16)
 
-    for h in range(2):
-        second(h, 0)
-    for h in range(2):
-        mid[h] = last(h, 0).astype(BF16)
-    for h in range(2):
-        first_far(h, 1)
-    for h in range(2):
-        first_near(h, 1)
-    for h in range(2):
-        second(h, 1)
-    for h in range(2):
-        stream[:, half_cols(h)] = last(h, 1) + resid_ref[:, half_cols(h)].astype(F32)
-    value = stream[...]
-    mean_square = jnp.mean(value * value, axis=1, keepdims=True)
-    nrm[...] = (value * lax.rsqrt(mean_square + 1e-06) * gain_ref[...].reshape(1, 3584)).astype(BF16)
-    for copy in started.values():
-        copy.wait_send()
-
-    LINE = ((0, 1), (1, 0), (3, 0), (1, 1), (3, 1), (2, 0), (2, 1))
-    for part, lo, n in PARTS:
-        cols = pl.ds(lo, n)
-        own = me.own_line(part) * 2 + me.c
-        for step, core in LINE:
-            to = me.line(part, up(me.own_line(part), step), lax.rem(me.c + core, 2))
-            send(nrm.at[:, cols], toks.at[own, :, cols], g_s.at[part], g_r.at[part], to)
-        pltpu.make_async_copy(nrm.at[:, cols], toks.at[own, :, cols], g_r.at[part]).start()
-
     def half_of(ref, half):
         if ref is part4:
             return lambda b1, b2, cols: part4.at[b1, b2, pl.ds(half * 16, 16), cols]
@@ -314,8 +209,8 @@
                 value = dot(swap[part - 1], stage[half, :, :, :, cols].reshape(256, n))
                 rows[half, :, :, :, cols] = value.astype(BF16).reshape(4, 4, 16, n)
         if half == 0:
-            loads[2].wait()
-            loads[3].wait()
+            loads[0].wait()
+            loads[1].wait()
 
         def hidden(j, carry):
             cols = pl.ds(pl.multiple_of(j * 256, 256), 256)
@@ -364,7 +259,7 @@
     for part, lo, n in PARTS:
         cols = pl.ds(lo, n)
         whole(recv.at[:, :, cols], c_r.at[part])
-        total = stream[:, cols]
+        total = stream_ref[:, cols]
         for q in range(8):
             total += recv[q, :, cols].astype(F32)
         out_ref[:, cols] = total.astype(BF16)
@@ -376,7 +271,7 @@
         whole(metas.at[part, pl.ds(0, 7)], m_s.at[part])
 
 
-def back(head_out, out_proj, resid, norm_gain, routes, weights, expert_in, expert_down):
+def back(stream, norm_gain, routes, weights, expert_in, expert_down):
     vmem = pl.BlockSpec(memory_space=pltpu.VMEM)
     hbm = pl.BlockSpec(memory_space=pl.ANY)
     dma = pltpu.SemaphoreType.DMA
@@ -384,30 +279,18 @@
     return pl.pallas_call(
         back_kernel,
         out_shape=jax.ShapeDtypeStruct((32, 3584), BF16),
-        in_specs=[hbm, hbm, vmem, vmem, vmem, vmem, hbm, hbm],
+        in_specs=[vmem, vmem, vmem, vmem, hbm, hbm],
         out_specs=vmem,
         scratch_shapes=[
-            pltpu.VMEM((4, 4, 32, 512), BF16),
-            pltpu.VMEM((4, 512, 896), BF16),
             pltpu.VMEM((3584, 2048), BF16),
             pltpu.VMEM((1024, 3584), BF16),
             pltpu.VMEM((4, 4, 32, 3584), BF16),
-            pltpu.VMEM((2, 4, 32, 896), BF16),
-            pltpu.VMEM((2, 4, 32, 896), BF16),
-            pltpu.VMEM((2, 4, 32, 1792), BF16),
-            pltpu.VMEM((2, 4, 32, 1792), BF16),
-            pltpu.VMEM((2, 4, 32, 1792), BF16),
-            pltpu.VMEM((2, 32, 896), BF16),
-            pltpu.VMEM((2, 32, 896), BF16),
-            pltpu.VMEM((2, 32, 1792), BF16),
-            pltpu.VMEM((2, 32, 1792), BF16),
             pltpu.VMEM((128, 128), F32),
             pltpu.VMEM((32, 128), F32),
             pltpu.VMEM((3, 8, 32, 128), F32),
             pltpu.VMEM((3, 2, 256, 256), BF16),
             pltpu.VMEM((3, 2, 256, 256), BF16),
             pltpu.VMEM((2, 256, 256), BF16),
-            pltpu.VMEM((32, 3584), F32),
             pltpu.VMEM((32, 3584), BF16),
             pltpu.VMEM((8, 32, 3584), BF16),
             pltpu.VMEM(halves, BF16),
@@ -417,9 +300,7 @@
             pltpu.VMEM((256, 3584), F32),
             pltpu.VMEM((8, 32, 3584), BF16),
             pltpu.VMEM((8, 32, 3584), BF16),
-            dma((4,)),
-            dma((24,)),
-            dma((24,)),
+            dma((2,)),
             dma((3,)),
             dma((3,)),
             dma((3,)),
@@ -435,17 +316,18 @@
             collective_id=1, has_side_effects=True, vmem_limit_bytes=67043328
         ),
         name="back",
-    )(head_out, out_proj, resid, norm_gain, routes, weights, expert_in, expert_down)
+    )(stream, norm_gain, routes, weights, expert_in, expert_down)
 
 
 LOWEST = -1e30
 
 
 def front_kernel(
-    scale, off_ref, q_ref, cache_ref, vup_ref, wot_ref,
-    ho_ref, wide_ref,
-    keys, kc, vt, qt, vupt, bias, scores, acc, top, tot, wo_ref, pair,
-    k_s, k_r, w_s, w_r, own_sem,
+    scale, off_ref, q_ref, cache_ref, vup_ref, wot_ref, resid_ref,
+    stream_ref,
+    keys, kc, vt, qt, vupt, bias, scores, probs, acc, top, tot, slabs, wide, ho,
+    part4, r1, l1, r2, l2, mid, r1b, l1b, r2b, l2b,
+    k_s, k_r, w_s, w_r, own_sem, rs_s, rs_r,
 ):
     me = Place()
     here = me.z * 2 + me.c
@@ -458,7 +340,7 @@
     own_copy = pltpu.make_async_copy(cache_ref, keys.at[me.x, me.y], own_sem)
     own_copy.start()
 
-    wo_ref[...] = wot_ref[...].T
+    slabs[me.z, me.c] = wot_ref[...].T
     twin = (me.z * 2 + 1 - me.c, me.x * 4 + me.y)
     above = [(up(me.z, n) * 2 + me.c, me.x * 4 + me.y) for n in (1, 3, 2)]
     others = [along(0, 1), along(0, 3), along(1, 1), along(1, 3), twin] + above
@@ -511,35 +393,31 @@
 
     for half in range(2):
         spread(half, 0)
-    send(wo_ref, pair, w_s.at[0], w_r.at[0], twin)
-
-    qt[:, pl.ds(576, 64), :] = jnp.zeros((4, 64, 512), BF16)
-    for h in range(2):
-        lo = h * 1152
-        qt[2 * h, pl.ds(0, 576), :] = q_ref[:, lo : lo + 640].T[:576]
-        qt[2 * h + 1, pl.ds(0, 576), :] = q_ref[:, lo + 512 : lo + 1152].T[64:]
+    mine = slabs.at[me.z, me.c]
+    send(mine, mine, w_s.at[0], w_r.at[0], twin)
+    for k, to in enumerate(above):
+        send(mine, mine, w_s.at[1 + k], w_r.at[1 + k], to)
+
+    qt[:, :, pl.ds(576, 64), :] = jnp.zeros((2, 2, 64, 512), BF16)
+    for tile in range(2):
+        for h in range(4):
+            lo = h * 576 - h % 2 * 64
+            some = q_ref[:, pl.ds(tile * 16, 16), lo : lo + 640].reshape(256, 640).T
+            lanes = pl.ds(h % 2 * 256, 256)
+            qt[tile, h // 2, pl.ds(0, 576), lanes] = some[64:] if h % 2 else some[:576]
     for half in range(2):
         forward(half, 0)
     for h in range(4):
         vupt[h] = vup_ref[h].T
-    kc[:, pl.ds(512, 128)] = jnp.zeros((768, 128), BF16)
-    top[...] = jnp.full((4, 1, 512), -3e38, F32)
-    tot[...] = jnp.zeros((4, 1, 512), F32)
-    acc[...] = jnp.zeros((4, 512, 512), F32)
-    whole(pair, w_r.at[0])
-    first = wo_ref[...]
-    second = pair[...]
-    low = jnp.where(me.c == 0, first, second)
-    high = jnp.where(me.c == 0, second, first)
-    wide_ref[me.z] = jnp.concatenate([low, high], axis=1)
+    kc[:, :, pl.ds(512, 128)] = jnp.zeros((4, 768, 128), BF16)
+    top[...] = jnp.full((2, 2, 1, 512), -3e38, F32)
+    tot[...] = jnp.zeros((2, 2, 1, 512), F32)
+    acc[...] = jnp.zeros((2, 2, 512, 512), F32)
     own_copy.wait()
     for half in range(2):
         far(half, 0)
     for half in range(2):
         spread(half, 1)
-    rows = pl.ds(pl.multiple_of(me.c * 256, 256), 256)
-    for k, to in enumerate(above):
-        send(wide_ref.at[me.z, rows], wide_ref.at[me.z, rows], w_s.at[1 + k], w_r.at[1 + k], to)
 
     row = lax.broadcasted_iota(I32, (768, 1), 0)
     in_first = row < 384
@@ -547,103 +425,228 @@
     nth = (low_row >= 96).astype(I32) + (low_row >= 192).astype(I32) + (low_row >= 288).astype(I32)
     low_row = low_row - nth * 96
     base = jnp.where(in_first, nth * 768 + low_row, nth * 192 + 96 + low_row)
-    query = lax.broadcasted_iota(I32, (768, 512), 1)
+    lane = lax.broadcasted_iota(I32, (768, 256), 1)
+    query = lane // 16 * 32 + lane % 16
+
+    def turn_of(chunk):
+        return chunk + lax.div(chunk, 2) - 2 * lax.div(chunk, 3)
+
+    def build(chunk):
+        turn = (0, 1, 3, 2)[chunk]
+        b, a = up(me.y, turn), up(me.x, turn)
+        kc[chunk, pl.ds(0, 384), pl.ds(0, 576)] = keys[:, b, pl.ds(0, 96), :].reshape(384, 576)
+        kc[chunk, pl.ds(384, 384), pl.ds(0, 576)] = keys[a, :, pl.ds(96, 96), :].reshape(384, 576)
+        vt[chunk] = kc[chunk, :, pl.ds(0, 512)].T
+
+    def finish(tile):
+        for g in range(2):
+            context = (acc[tile, g] / tot[tile, g]).astype(BF16)
+            for k in range(2):
+                value = dot(vupt[2 * g + k], context[:, k * 256 : k * 256 + 256]).T.astype(BF16)
+                ho[tile, :, :, :, pl.ds((2 * g + k) * 128, 128)] = value.reshape(4, 4, 16, 128)
+        for h in range(2):
+            for b in range(2):
+                value = dot(ho[tile].reshape(256, 512), wide[2 * h + b])
+                cols = pl.ds(h * 1792 + b * 896, 896)
+                part4[tile, :, :, :, cols] = value.astype(BF16).reshape(4, 4, 16, 896)
+
+    def position(h, phase):
+        return me.x if h == phase else me.y
+
+    def piece(tile, h, phase, k, lo, n):
+        if phase:
+            return mid.at[tile, h, k, :, pl.ds(lo, n)]
+        cols = pl.ds(h * 1792 + lo, n)
+        return part4.at[tile, :, k, :, cols] if h else part4.at[tile, k, :, :, cols]
+
+    def box(i, tile, h, phase, lo, n):
+        ref = (r1b, l1b, r2b, l2b)[i] if phase else (r1, l1, r2, l2)[i]
+        if phase:
+            return ref.at[tile, h, :, pl.ds(lo, n)]
+        return ref.at[tile, h, :, :, pl.ds(lo, n)]
+
+    def rs_sem(tile, h, phase, k):
+        return ((tile * 2 + h) * 2 + phase) * 6 + k
+
+    def give(tile, h, phase, k, src, dst, n):
+        i = rs_sem(tile, h, phase, k)
+        send(src, dst, rs_s.at[i], rs_r.at[i], along(0 if h == phase else 1, n))
+
+    def first(tile, phase):
+        for h in range(2):
+            for side, (lo, n) in enumerate(((0, 1), (896, 3))):
+                src = piece(tile, h, phase, up(position(h, phase), 2), lo, 896)
+                give(tile, h, phase, side, src, box(side, tile, h, phase, 0, 896), n)
+        for h in range(2):
+            for side, (lo, n) in enumerate(((896, 1), (0, 3))):
+                src = piece(tile, h, phase, up(position(h, phase), n), lo, 896)
+                give(tile, h, phase, 2 + side, src, box(2 + side, tile, h, phase, lo, 896), n)
+
+    def second(tile, phase):
+        for h in range(2):
+            for side, (lo, n) in enumerate(((0, 1), (896, 3))):
+                came = box(side, tile, h, phase, 0, 896)
+                whole(came, rs_r.at[rs_sem(tile, h, phase, side)])
+                own = piece(tile, h, phase, up(position(h, phase), n), lo, 896)
+                own[...] = (own[...].astype(F32) + came[...].astype(F32)).astype(BF16)
+                give(tile, h, phase, 4 + side, own, box(2 + side, tile, h, phase, lo, 896), n)
+
+    def last(tile, h, phase):
+        for k, (side, lo) in enumerate(((2, 896), (3, 0), (2, 0), (3, 896))):
+            whole(box(side, tile, h, phase, lo, 896), rs_r.at[rs_sem(tile, h, phase, 2 + k)])
+        total = piece(tile, h, phase, position(h, phase), 0, 1792)[...].astype(F32)
+        total += box(2, tile, h, phase, 0, 1792)[...].astype(F32)
+        return total + box(3, tile, h, phase, 0, 1792)[...].astype(F32)
+
+    def middle(tile):
+        for h in range(2):
+            mid[tile, h] = last(tile, h, 0).astype(BF16)
+        first(tile, 1)
+
+    def settle(tile):
+        rows, cols = pl.ds(tile * 16, 16), (pl.ds(0, 1792), pl.ds(1792, 1792))
+        for h in range(2):
+            stream_ref[rows, cols[h]] = last(tile, h, 1) + resid_ref[rows, cols[h]].astype(F32)
+
+    build(0)
 
     def step(i, carry):
         @pl.when(i == 1)
         def _():
             for half in range(2):
                 forward(half, 1)
-
-        @pl.when(i == 3)
+            build(1)
+            build(2)
+
+        @pl.when(i == 2)
         def _():
             for half in range(2):
                 far(half, 1)
+            build(3)
             for k, n in enumerate((3, 1, 2)):
-                z = up(me.z, n)
-                got = wide_ref.at[z, rows]
+                got = slabs.at[up(me.z, n), me.c]
                 whole(got, w_r.at[1 + k])
                 send(got, got, w_s.at[4 + k], w_r.at[4 + k], twin)
 
-        turn = i + lax.div(i, 2) - 2 * lax.div(i, 3)
-        b, a = up(me.y, turn), up(me.x, turn)
-        kc[pl.ds(0, 384), pl.ds(0, 576)] = keys[:, b, pl.ds(0, 96), :].reshape(384, 576)
-        kc[pl.ds(384, 384), pl.ds(0, 576)] = keys[a, :, pl.ds(96, 96), :].reshape(384, 576)
+        @pl.when(i == 3)
+        def _():
+            whole(slabs.at[me.z, 1 - me.c], w_r.at[0])
+            for k, n in enumerate((3, 1, 2)):
+                whole(slabs.at[up(me.z, n), 1 - me.c], w_r.at[4 + k])
+            for z in range(4):
+                wide[z] = jnp.concatenate([slabs[z, 0], slabs[z, 1]], axis=1)
+            finish(0)
+            first(0, 0)
+
+        tiles = (lax.div(i, 3), jnp.where(i == 1, 0, 1))
+        chunks = (turn_of(i), jnp.where(i == 1, 2, jnp.where(i == 2, 1, i)))
 
         def score(u):
-            scores[u % 2] = dot(kc[...], qt[u])
+            scores[u % 2] = dot(kc[chunks[u // 2]], qt[tiles[u // 2], u % 2])
 
         score(0)
-        vt[...] = kc[:, pl.ds(0, 512)].T
-        start = jnp.where(in_first, b * 192, a * 768)
-        bias[...] = jnp.where(base + start - off_ref[0] <= query, 0.0, LOWEST)
-        for h in range(4):
-            if h < 3:
-                score(h + 1)
-            s = scores[h % 2] * scale + bias[...]
-            old = top[h]
-            new = jnp.maximum(old, jnp.max(s, axis=0, keepdims=True))
-            p = jnp.exp2(s - new)
-            shrink = jnp.exp2(old - new)
-            top[h] = new
-            tot[h] = tot[h] * shrink + jnp.sum(p, axis=0, keepdims=True)
-            acc[h] = acc[h] * shrink + dot(vt[...], p.astype(BF16))
+        for u in range(4):
+            tile, g = tiles[u // 2], u % 2
+            if u < 3:
+                score(u + 1)
+            if g == 0:
+                turn = turn_of(chunks[u // 2])
+                start = jnp.where(in_first, up(me.y, turn) * 192, up(me.x, turn) * 768)
+                limit = query + (tile * 16 + off_ref[0])
+                bias[...] = jnp.where(base + start <= limit, 0.0, LOWEST)
+            for k in range(2):
+                lanes = pl.ds(k * 256, 256)
+                s = scores[g, :, lanes] * scale + bias[...]
+                old = top[tile, g, :, lanes]
+                new = jnp.maximum(old, jnp.max(s, axis=0, keepdims=True))
+                p = jnp.exp2(s - new)
+                shrink = jnp.exp2(old - new)
+                top[tile, g, :, lanes] = new
+                tot[tile, g, :, lanes] = tot[tile, g, :, lanes] * shrink + jnp.sum(p, axis=0, keepdims=True)
+                acc[tile, g, :, lanes] = acc[tile, g, :, lanes] * shrink
+                probs[g, :, lanes] = p.astype(BF16)
+            acc[tile, g] += dot(vt[chunks[u // 2]], probs[g])
+            if u == 1:
+
+                @pl.when(i == 3)
+                def _():
+                    second(0, 0)
+
         return carry
 
     lax.fori_loop(0, 4, step, 0)
-    for h in range(4):
-        context = (acc[h] / tot[h]).astype(BF16)
-        value = dot(vupt[h], context).T.astype(BF16)
-        ho_ref[:, :, :, pl.ds(h * 128, 128)] = value.reshape(4, 4, 32, 128)
-    rest = pl.ds(pl.multiple_of(256 - me.c * 256, 256), 256)
+    middle(0)
+    finish(1)
+    first(1, 0)
+    second(0, 1)
+    second(1, 0)
+    settle(0)
+    middle(1)
+    second(1, 1)
+    settle(1)
     for k, n in enumerate((3, 1, 2)):
-        z = up(me.z, n)
-        whole(wide_ref.at[z, rest], w_r.at[4 + k])
-        whole(wide_ref.at[z, rows], w_s.at[4 + k])
-        whole(wide_ref.at[me.z, rows], w_s.at[1 + k])
-    whole(wo_ref, w_s.at[0])
+        whole(mine, w_s.at[1 + k])
+        whole(slabs.at[up(me.z, n), me.c], w_s.at[4 + k])
+    whole(mine, w_s.at[0])
     for half in range(2):
         for phase in range(2):
             for k in range(2):
                 whole(spot(half, phase, 0, 0, 96), k_s.at[sem(half, phase, k)])
                 whole(spot(half, phase, 0, 0, 48), k_s.at[sem(half, phase, 2 + k)])
-
-
-def front(offsets, queries, cache, value_up, out_proj, scale):
+    for tile in range(2):
+        for h in range(2):
+            for phase in range(2):
+                for k in range(6):
+                    src = piece(tile, h, phase, 0, 0, 896)
+                    whole(src, rs_s.at[rs_sem(tile, h, phase, k)])
+
+
+def front(offsets, queries, cache, value_up, out_proj, resid, scale):
     vmem = pl.BlockSpec(memory_space=pltpu.VMEM)
     dma = pltpu.SemaphoreType.DMA
     return pl.pallas_call(
         functools.partial(front_kernel, scale),
-        out_shape=(
-            jax.ShapeDtypeStruct((4, 4, 32, 512), BF16),
-            jax.ShapeDtypeStruct((4, 512, 896), BF16),
-        ),
-        in_specs=[pl.BlockSpec(memory_space=pltpu.SMEM), vmem, vmem, vmem, vmem],
-        out_specs=(vmem, vmem),
+        out_shape=jax.ShapeDtypeStruct((32, 3584), F32),
+        in_specs=[pl.BlockSpec(memory_space=pltpu.SMEM), vmem, vmem, vmem, vmem, vmem],
+        out_specs=vmem,
         scratch_shapes=[
             pltpu.VMEM((4, 4, 192, 576), BF16),
-            pltpu.VMEM((768, 640), BF16),
-            pltpu.VMEM((512, 768), BF16),
-            pltpu.VMEM((4, 640, 512), BF16),
+            pltpu.VMEM((4, 768, 640), BF16),
+            pltpu.VMEM((4, 512, 768), BF16),
+            pltpu.VMEM((2, 2, 640, 512), BF16),
             pltpu.VMEM((4, 128, 512), BF16),
-            pltpu.VMEM((768, 512), F32),
+            pltpu.VMEM((768, 256), F32),
             pltpu.VMEM((2, 768, 512), F32),
-            pltpu.VMEM((4, 512, 512), F32),
-            pltpu.VMEM((4, 1, 512), F32),
-            pltpu.VMEM((4, 1, 512), F32),
-            pltpu.VMEM((512, 448), BF16),
-            pltpu.VMEM((512, 448), BF16),
+            pltpu.VMEM((2, 768, 512), BF16),
+            pltpu.VMEM((2, 2, 512, 512), F32),
+            pltpu.VMEM((2, 2, 1, 512), F32),
+            pltpu.VMEM((2, 2, 1, 512), F32),
+            pltpu.VMEM((4, 2, 512, 448), BF16),
+            pltpu.VMEM((4, 512, 896), BF16),
+            pltpu.VMEM((2, 4, 4, 16, 512), BF16),
+            pltpu.VMEM((2, 4, 4, 16, 3584), BF16),
+            pltpu.VMEM((2, 2, 4, 16, 896), BF16),
+            pltpu.VMEM((2, 2, 4, 16, 896), BF16),
+            pltpu.VMEM((2, 2, 4, 16, 1792), BF16),
+            pltpu.VMEM((2, 2, 4, 16, 1792), BF16),
+            pltpu.VMEM((2, 2, 4, 16, 1792), BF16),
+            pltpu.VMEM((2, 2, 16, 896), BF16),
+            pltpu.VMEM((2, 2, 16, 896), BF16),
+            pltpu.VMEM((2, 2, 16, 1792), BF16),
+            pltpu.VMEM((2, 2, 16, 1792), BF16),
             dma((16,)),
             dma((16,)),
             dma((7,)),
             dma((7,)),
             dma(()),
+            dma((48,)),
+            dma((48,)),
         ],
         compiler_params=pltpu.CompilerParams(
-            collective_id=2, has_side_effects=True, vmem_limit_bytes=60 * 1024 * 1024
+            collective_id=2, has_side_effects=True, vmem_limit_bytes=67043328
         ),
         name="front",
-    )(offsets, queries, cache, value_up, out_proj)
+    )(offsets, queries, cache, value_up, out_proj, resid)
 
 
 def shards(
@@ -662,12 +665,11 @@
     latent_width = value_up.shape[1]
     key_width = cache.shape[2]
     score_scale = (value_up.shape[2] + key_width - latent_width) ** (-0.5)
-    head_out, wide = front(
-        offsets, queries, cache[0], value_up, out_proj.T, score_scale * LOG2_E
+    stream = front(
+        offsets, queries.reshape(16, 32, -1), cache[0], value_up, out_proj.T, resid,
+        score_scale * LOG2_E,
     )
-    return back(
-        head_out, wide, resid, norm_gain, routes.T, route_weights.T, expert_in[0], expert_down[0]
-    )
+    return back(stream, norm_gain, routes.T, route_weights.T, expert_in[0], expert_down[0])
 
 
 def solution(mesh):

time: 162 us -> 164 us (1.012)
    pallas_call x1, Pallas kernels: 45.3 us -> 68.8 us  [front(): pl.pallas_call(functools.partial(front_kernel, scale), out_shape=jax.Shap...]
    pallas_call x1, Pallas kernels: 115 us -> 92.6 us  [back(): pl.pallas_call(back_kernel, out_shape=jax.ShapeDtypeStruct((32, 3584), BF...]
where the time goes in v4:
time: 164 us
  Pallas kernels  161 us (98%)
    pallas_call x1, Pallas kernels, back(): pl.pallas_call(back_kernel, out_shape=jax.ShapeDtypeStruct((32, 3584), BF...  92.6 us
    pallas_call x1, Pallas kernels, front(): pl.pallas_call(functools.partial(front_kernel, scale), out_shape=jax.Shap...  68.8 us

profile of v4, /device:TPU:1, one launch (start us, length us, event | category | flops | bytes accessed | tf_op | source)
XLA Modules:
  0.0 163.7 jit_solution(7928995660565719815)
XLA Ops:
  0.7 68.8 %front.1.stream_ref = f32[32,3584]{1,0:T(8,128)} custom-call(s32[1]{0:T(128)S(6)} %copy.13.off_ref, bf16[16,32,2304]{2,1,0:T(8,128)(2,1)} %bitcast.9, bf16[192,576]{1,0:T(8,128)(2,1)} %bitcast.11, bf16[4,512,128]{2,1,0:T(8,128)(2,1)} %vup_ref.1, bf16[448,512]{1,0:T(8,128)(2,1)} %bitcast.10, bf16[32,3584]{1,0:T(8,128)(2,1)} %resid_ref.1), custom_call_target="tpu_custom_call" | custom-call | tf_op jit(solution)/shard_map/front/pallas_call | solution.py:607
  69.5 92.6 %back.1 = bf16[32,3584]{1,0:T(8,128)(2,1)} custom-call(f32[32,3584]{1,0:T(8,128)} %front.1.stream_ref, f32[3584]{0:T(1024)} %gain_ref.1, s32[8,32]{1,0:T(8,128)} %bitcast.12, f32[8,32]{1,0:T(8,128)} %bitcast.13, bf16[3584,2048]{1,0:T(8,128)(2,1)} %bitcast.7, bf16[1024,3584]{1,0:T(8,128)(2,1)} %bitcast.8), custom_call_target="tpu_custom_call" | custom-call | tf_op jit(solution)/shard_map/back/pallas_call | solution.py:279
  162.1 1.6 %copy.14 = bf16[32,3584]{1,0:T(8,128)(2,1)} copy(bf16[32,3584]{1,0:T(8,128)(2,1)} %back.1) | data formatting | bytes 458752

commit v5 on v4

--- a/solution.py
+++ b/solution.py
@@ -81,8 +81,8 @@
     stream_ref, gain_ref, routes_ref, weights_ref, win_hbm, wdown_hbm,
     out_ref,
     win, wdown, part4, turned, table_ref, metas, pick, wgt, swap,
-    nrm, toks, outg, rows, stage, hid, half_sum, psum, recv,
-    wsem, m_s, m_r, g_s, g_r, d_s, d_r, t_s, t_r, c_s, c_r,
+    nrm, toks, outg, rows, stage, hid, half_sum, psum, other_core, recv,
+    wsem, m_s, m_r, g_s, g_r, d_s, d_r, t_s, t_r, x_s, x_r, c_s, c_r,
 ):
     me = Place()
     barrier = pltpu.get_barrier_semaphore()
@@ -123,14 +123,22 @@
                 meta_sends.append(send(table_ref, metas.at[part, own], m_s.at[part], m_r.at[part], to))
         pltpu.make_async_copy(table_ref, metas.at[part, own], m_r.at[part]).start()
 
-    LINE = ((0, 1), (1, 0), (3, 0), (1, 1), (3, 1), (2, 0), (2, 1))
+    def to_line(part, n):
+        return me.line(part, up(me.own_line(part), n), me.c)
+
+    twin = (me.z * 2 + 1 - me.c, me.x * 4 + me.y)
     for part, lo, n in PARTS:
-        cols = pl.ds(lo, n)
-        own = me.own_line(part) * 2 + me.c
-        for step, core in LINE:
-            to = me.line(part, up(me.own_line(part), step), lax.rem(me.c + core, 2))
-            send(nrm.at[:, cols], toks.at[own, :, cols], g_s.at[part], g_r.at[part], to)
-        pltpu.make_async_copy(nrm.at[:, cols], toks.at[own, :, cols], g_r.at[part]).start()
+        spot = (me.own_line(part), me.c, slice(None), pl.ds(lo, n))
+        toks[spot] = nrm[:, pl.ds(lo, n)]
+        for k, step in enumerate((1, 3, 2)):
+            send(nrm.at[:, pl.ds(lo, n)], toks.at[spot], g_s.at[part], g_r.at[part * 4 + k], to_line(part, step))
+        send(nrm.at[:, pl.ds(lo, n)], toks.at[spot], g_s.at[part], g_r.at[part * 4 + 3], twin)
+
+    def pass_on(k):
+        for part, lo, n in PARTS:
+            got = toks.at[up(me.own_line(part), (3, 1, 2)[k]), me.c, :, pl.ds(lo, n)]
+            whole(got, g_r.at[part * 4 + k])
+            send(got, got, g_s.at[part], g_r.at[part * 4 + 3], twin)
 
     token = lax.broadcasted_iota(I32, (256, 256), 0)
     other = lax.broadcasted_iota(I32, (256, 256), 1)
@@ -158,6 +166,10 @@
             chosen = rank == half * 2.0
             pick[part, half] = jnp.where(chosen, 1.0, 0.0).T.astype(BF16)
             wgt[part, half] = jnp.where(chosen, weight, 0.0).astype(BF16)
+        if part == 1:
+            pass_on(0)
+            pass_on(1)
+    pass_on(2)
     rx, ry, rz, low = token // 64, token // 16 % 4, token // 4 % 4, token % 4
     swap[0] = jnp.where(other == rz * 64 + ry * 16 + rx * 4 + low, 1.0, 0.0).astype(BF16)
     swap[1] = jnp.where(other == rx * 64 + rz * 16 + ry * 4 + low, 1.0, 0.0).astype(BF16)
@@ -196,8 +208,8 @@
         for part, lo, n in PARTS:
             cols = pl.ds(lo, n)
             if half == 0:
-                whole(toks.at[:, :, cols], g_r.at[part])
-            value = dot(pick[part, half], toks[:, :, cols].reshape(256, n))
+                whole(toks.at[:, 1 - me.c, :, cols], g_r.at[part * 4 + 3])
+            value = dot(pick[part, half], toks[:, :, :, cols].reshape(256, n))
             outg[half, :, :, :, cols] = value.astype(BF16).reshape(4, 4, 16, n)
         exchange(half, outg, landing, d_s, d_r, PARTS)
 
@@ -247,27 +259,35 @@
             if half == 0:
                 half_sum[:, cols] = value
                 continue
-            psum[:, :, cols] = (half_sum[:, cols] + value).astype(BF16).reshape(8, 32, n)
-            own = me.own_line(part) * 2 + me.c
-            for step, core in LINE:
-                a, k = up(me.own_line(part), step), lax.rem(me.c + core, 2)
-                send(
-                    psum.at[a * 2 + k, :, cols], recv.at[own, :, cols],
-                    c_s.at[part], c_r.at[part], me.line(part, a, k),
-                )
-            pltpu.make_async_copy(psum.at[own, :, cols], recv.at[own, :, cols], c_r.at[part]).start()
+            psum[:, :, :, cols] = (half_sum[:, cols] + value).astype(BF16).reshape(4, 2, 32, n)
+            send(psum.at[:, 1 - me.c, :, cols], other_core.at[:, :, cols], x_s.at[part], x_r.at[part], twin)
+    for part, lo, n in PARTS:
+        cols = pl.ds(lo, n)
+        own = me.own_line(part)
+        whole(other_core.at[:, :, cols], x_r.at[part])
+        both = psum[:, me.c, :, cols].astype(F32) + other_core[:, :, cols].astype(F32)
+        psum[:, me.c, :, cols] = both.astype(BF16)
+        for step in (1, 3, 2):
+            send(
+                psum.at[up(own, step), me.c, :, cols], recv.at[own, :, cols],
+                c_s.at[part], c_r.at[part], to_line(part, step),
+            )
+        pltpu.make_async_copy(psum.at[own, me.c, :, cols], recv.at[own, :, cols], c_r.at[part]).start()
     for part, lo, n in PARTS:
         cols = pl.ds(lo, n)
         whole(recv.at[:, :, cols], c_r.at[part])
         total = stream_ref[:, cols]
-        for q in range(8):
+        for q in range(4):
             total += recv[q, :, cols].astype(F32)
-        out_ref[:, cols] = total.astype(BF16)
+        out_ref[:, cols] = total
     for part, lo, n in PARTS:
+        cols = pl.ds(lo, n)
         for half in range(2):
             sent(half, lo, n, t_s.at[half * 3 + part])
-        whole(toks.at[pl.ds(0, 7), :, pl.ds(lo, n)], g_s.at[part])
-        whole(psum.at[pl.ds(0, 7), :, pl.ds(lo, n)], c_s.at[part])
+        whole(toks.at[pl.ds(0, 3), :, :, cols], g_s.at[part])
+        whole(nrm.at[:, cols], g_s.at[part])
+        whole(other_core.at[:, :, cols], x_s.at[part])
+        whole(recv.at[pl.ds(0, 3), :, cols], c_s.at[part])
         whole(metas.at[part, pl.ds(0, 7)], m_s.at[part])
 
 
@@ -278,7 +298,7 @@
     halves = (2, 4, 4, 16, 3584)
     return pl.pallas_call(
         back_kernel,
-        out_shape=jax.ShapeDtypeStruct((32, 3584), BF16),
+        out_shape=jax.ShapeDtypeStruct((32, 3584), F32),
         in_specs=[vmem, vmem, vmem, vmem, hbm, hbm],
         out_specs=vmem,
         scratch_shapes=[
@@ -292,23 +312,26 @@
             pltpu.VMEM((3, 2, 256, 256), BF16),
             pltpu.VMEM((2, 256, 256), BF16),
             pltpu.VMEM((32, 3584), BF16),
-            pltpu.VMEM((8, 32, 3584), BF16),
+            pltpu.VMEM((4, 2, 32, 3584), BF16),
             pltpu.VMEM(halves, BF16),
             pltpu.VMEM(halves, BF16),
             pltpu.VMEM(halves, BF16),
             pltpu.VMEM((3, 256, 1024), BF16),
             pltpu.VMEM((256, 3584), F32),
-            pltpu.VMEM((8, 32, 3584), BF16),
-            pltpu.VMEM((8, 32, 3584), BF16),
+            pltpu.VMEM((4, 2, 32, 3584), BF16),
+            pltpu.VMEM((4, 32, 3584), BF16),
+            pltpu.VMEM((4, 32, 3584), BF16),
             dma((2,)),
             dma((3,)),
             dma((3,)),
             dma((3,)),
-            dma((3,)),
+            dma((12,)),
             dma((6,)),
             dma((6,)),
             dma((6,)),
             dma((6,)),
+            dma((3,)),
+            dma((3,)),
             dma((3,)),
             dma((3,)),
         ],
@@ -438,17 +461,18 @@
         kc[chunk, pl.ds(384, 384), pl.ds(0, 576)] = keys[a, :, pl.ds(96, 96), :].reshape(384, 576)
         vt[chunk] = kc[chunk, :, pl.ds(0, 512)].T
 
-    def finish(tile):
+    def heads(tile):
         for g in range(2):
             context = (acc[tile, g] / tot[tile, g]).astype(BF16)
             for k in range(2):
                 value = dot(vupt[2 * g + k], context[:, k * 256 : k * 256 + 256]).T.astype(BF16)
                 ho[tile, :, :, :, pl.ds((2 * g + k) * 128, 128)] = value.reshape(4, 4, 16, 128)
-        for h in range(2):
-            for b in range(2):
-                value = dot(ho[tile].reshape(256, 512), wide[2 * h + b])
-                cols = pl.ds(h * 1792 + b * 896, 896)
-                part4[tile, :, :, :, cols] = value.astype(BF16).reshape(4, 4, 16, 896)
+
+    def project(tile, h):
+        for b in range(2):
+            value = dot(ho[tile].reshape(256, 512), wide[2 * h + b])
+            cols = pl.ds(h * 1792 + b * 896, 896)
+            part4[tile, :, :, :, cols] = value.astype(BF16).reshape(4, 4, 16, 896)
 
     def position(h, phase):
         return me.x if h == phase else me.y
@@ -472,15 +496,23 @@
         i = rs_sem(tile, h, phase, k)
         send(src, dst, rs_s.at[i], rs_r.at[i], along(0 if h == phase else 1, n))
 
-    def first(tile, phase):
+    def first_far(tile, h, phase):
+        for side, (lo, n) in enumerate(((0, 1), (896, 3))):
+            src = piece(tile, h, phase, up(position(h, phase), 2), lo, 896)
+            give(tile, h, phase, side, src, box(side, tile, h, phase, 0, 896), n)
+
+    def first_near(tile, h, phase):
+        for side, (lo, n) in enumerate(((896, 1), (0, 3))):
+            src = piece(tile, h, phase, up(position(h, phase), n), lo, 896)
+            give(tile, h, phase, 2 + side, src, box(2 + side, tile, h, phase, lo, 896), n)
+
+    def finish(tile):
+        heads(tile)
         for h in range(2):
-            for side, (lo, n) in enumerate(((0, 1), (896, 3))):
-                src = piece(tile, h, phase, up(position(h, phase), 2), lo, 896)
-                give(tile, h, phase, side, src, box(side, tile, h, phase, 0, 896), n)
+            project(tile, h)
+            first_far(tile, h, 0)
         for h in range(2):
-            for side, (lo, n) in enumerate(((896, 1), (0, 3))):
-                src = piece(tile, h, phase, up(position(h, phase), n), lo, 896)
-                give(tile, h, phase, 2 + side, src, box(2 + side, tile, h, phase, lo, 896), n)
+            first_near(tile, h, 0)
 
     def second(tile, phase):
         for h in range(2):
@@ -501,7 +533,10 @@
     def middle(tile):
         for h in range(2):
             mid[tile, h] = last(tile, h, 0).astype(BF16)
-        first(tile, 1)
+        for h in range(2):
+            first_far(tile, h, 1)
+        for h in range(2):
+            first_near(tile, h, 1)
 
     def settle(tile):
         rows, cols = pl.ds(tile * 16, 16), (pl.ds(0, 1792), pl.ds(1792, 1792))
@@ -536,19 +571,24 @@
             for z in range(4):
                 wide[z] = jnp.concatenate([slabs[z, 0], slabs[z, 1]], axis=1)
             finish(0)
-            first(0, 0)
 
         tiles = (lax.div(i, 3), jnp.where(i == 1, 0, 1))
         chunks = (turn_of(i), jnp.where(i == 1, 2, jnp.where(i == 2, 1, i)))
 
         def score(u):
             scores[u % 2] = dot(kc[chunks[u // 2]], qt[tiles[u // 2], u % 2])
+
+        def gather_values(u):
+            tile, g = tiles[u // 2], u % 2
+            acc[tile, g] += dot(vt[chunks[u // 2]], probs[g])
 
         score(0)
         for u in range(4):
             tile, g = tiles[u // 2], u % 2
             if u < 3:
                 score(u + 1)
+            if u > 0:
+                gather_values(u - 1)
             if g == 0:
                 turn = turn_of(chunks[u // 2])
                 start = jnp.where(in_first, up(me.y, turn) * 192, up(me.x, turn) * 768)
@@ -565,19 +605,18 @@
                 tot[tile, g, :, lanes] = tot[tile, g, :, lanes] * shrink + jnp.sum(p, axis=0, keepdims=True)
                 acc[tile, g, :, lanes] = acc[tile, g, :, lanes] * shrink
                 probs[g, :, lanes] = p.astype(BF16)
-            acc[tile, g] += dot(vt[chunks[u // 2]], probs[g])
             if u == 1:
 
                 @pl.when(i == 3)
                 def _():
                     second(0, 0)
 
+        gather_values(3)
         return carry
 
     lax.fori_loop(0, 4, step, 0)
     middle(0)
     finish(1)
-    first(1, 0)
     second(0, 1)
     second(1, 0)
     settle(0)
@@ -669,7 +708,8 @@
         offsets, queries.reshape(16, 32, -1), cache[0], value_up, out_proj.T, resid,
         score_scale * LOG2_E,
     )
-    return back(stream, norm_gain, routes.T, route_weights.T, expert_in[0], expert_down[0])
+    mixed = back(stream, norm_gain, routes.T, route_weights.T, expert_in[0], expert_down[0])
+    return mixed.astype(BF16)
 
 
 def solution(mesh):

time: 164 us -> 161 us (0.982)
  Pallas kernels: 161 us -> 158 us
  other arithmetic: 0 us -> 1.73 us
    pallas_call x1, Pallas kernels: 92.6 us -> 89.5 us  [back(): pl.pallas_call(back_kernel, out_shape=jax.ShapeDtypeStruct((32, 3584), F3...]
    convert_element_type x0 -> x1, other arithmetic: none -> 1.73 us  [shards(): return mixed.astype(BF16)]
    unnamed x1 -> x0, local copies, waits for them, and re-layouts: 1.64 us -> none
where the time goes in v5:
time: 161 us
  Pallas kernels  158 us (98%)
  other arithmetic  1.73 us (1%)
    pallas_call x1, Pallas kernels, back(): pl.pallas_call(back_kernel, out_shape=jax.ShapeDtypeStruct((32, 3584), F3...  89.5 us
    pallas_call x1, Pallas kernels, front(): pl.pallas_call(functools.partial(front_kernel, scale), out_shape=jax.Shap...  68.8 us

profile of v5, /device:TPU:1, one launch (start us, length us, event | category | flops | bytes accessed | tf_op | source)
XLA Modules:
  0.0 160.7 jit_solution(4721256793095568125)
XLA Ops:
  0.7 68.8 %front.1.stream_ref = f32[32,3584]{1,0:T(8,128)} custom-call(s32[1]{0:T(128)S(6)} %copy.12.off_ref, bf16[16,32,2304]{2,1,0:T(8,128)(2,1)} %bitcast.9, bf16[192,576]{1,0:T(8,128)(2,1)} %bitcast.11, bf16[4,512,128]{2,1,0:T(8,128)(2,1)} %vup_ref.1, bf16[448,512]{1,0:T(8,128)(2,1)} %bitcast.10, bf16[32,3584]{1,0:T(8,128)(2,1)} %resid_ref.1), custom_call_target="tpu_custom_call" | custom-call | tf_op jit(solution)/shard_map/front/pallas_call | solution.py:646
  69.4 89.5 %back.1 = f32[32,3584]{1,0:T(8,128)} custom-call(f32[32,3584]{1,0:T(8,128)} %front.1.stream_ref, f32[3584]{0:T(1024)} %gain_ref.1, s32[8,32]{1,0:T(8,128)} %bitcast.12, f32[8,32]{1,0:T(8,128)} %bitcast.13, bf16[3584,2048]{1,0:T(8,128)(2,1)} %bitcast.7, bf16[1024,3584]{1,0:T(8,128)(2,1)} %bitcast.8), custom_call_target="tpu_custom_call" | custom-call | tf_op jit(solution)/shard_map/back/pallas_call | solution.py:299
  158.9 1.7 %convert_element_type.3 = bf16[32,3584]{1,0:T(8,128)(2,1)} convert(f32[32,3584]{1,0:T(8,128)} %back.1) | non-fusion elementwise | flops 114688 | bytes 688128 | tf_op jit(solution)/shard_map/convert_element_type | solution.py:712

commit v6 on v5

--- a/solution.py
+++ b/solution.py
@@ -348,7 +348,7 @@
 def front_kernel(
     scale, off_ref, q_ref, cache_ref, vup_ref, wot_ref, resid_ref,
     stream_ref,
-    keys, kc, vt, qt, vupt, bias, scores, probs, acc, top, tot, slabs, wide, ho,
+    keys, kc, vt, qt, vupt, places, bias, scores, probs, acc, top, tot, slabs, wide, ho,
     part4, r1, l1, r2, l2, mid, r1b, l1b, r2b, l2b,
     k_s, k_r, w_s, w_r, own_sem, rs_s, rs_r,
 ):
@@ -383,36 +383,37 @@
     def axis_of(half, phase):
         return half if phase == 0 else 1 - half
 
-    def spot(half, phase, n, lo, rows):
+    def spot(half, phase, n, lo, rows, part=0):
         rows = pl.ds(half * 96 + lo, rows)
+        two = pl.ds(part * 2, 2)
         if axis_of(half, phase) == 0:
             a = up(me.x, n)
-            return keys.at[a, me.y, rows] if phase == 0 else keys.at[a, :, rows]
+            return keys.at[a, me.y, rows] if phase == 0 else keys.at[a, two, rows]
         b = up(me.y, n)
-        return keys.at[me.x, b, rows] if phase == 0 else keys.at[:, b, rows]
-
-    def sem(half, phase, k):
-        return (half * 2 + phase) * 4 + k
-
-    def spread(half, phase):
+        return keys.at[me.x, b, rows] if phase == 0 else keys.at[two, b, rows]
+
+    def sem(half, phase, k, part=0):
+        return half * 12 + phase * 4 + part * 4 + k
+
+    def spread(half, phase, part=0):
         axis = axis_of(half, phase)
         for k, n in ((0, 1), (1, 3)):
-            at = spot(half, phase, 0, 0, 96)
+            at = spot(half, phase, 0, 0, 96, part)
             src = cache_ref.at[pl.ds(half * 96, 96)] if phase == 0 else at
-            i = sem(half, phase, k)
+            i = sem(half, phase, k, part)
             send(src, at, k_s.at[i], k_r.at[i], along(axis, n))
 
-    def forward(half, phase):
+    def forward(half, phase, part=0):
         axis = axis_of(half, phase)
         for k, n, lo in ((0, 3, 0), (1, 1, 48)):
-            whole(spot(half, phase, n, 0, 96), k_r.at[sem(half, phase, k)])
-            part = spot(half, phase, n, lo, 48)
-            i = sem(half, phase, 2 + k)
-            send(part, part, k_s.at[i], k_r.at[i], along(axis, 4 - n))
-
-    def far(half, phase):
+            whole(spot(half, phase, n, 0, 96, part), k_r.at[sem(half, phase, k, part)])
+            some = spot(half, phase, n, lo, 48, part)
+            i = sem(half, phase, 2 + k, part)
+            send(some, some, k_s.at[i], k_r.at[i], along(axis, 4 - n))
+
+    def far(half, phase, part=0):
         for k, lo in ((0, 0), (1, 48)):
-            whole(spot(half, phase, 2, lo, 48), k_r.at[sem(half, phase, 2 + k)])
+            whole(spot(half, phase, 2, lo, 48, part), k_r.at[sem(half, phase, 2 + k, part)])
 
     for half in range(2):
         spread(half, 0)
@@ -439,31 +440,44 @@
     own_copy.wait()
     for half in range(2):
         far(half, 0)
-    for half in range(2):
-        spread(half, 1)
-
-    row = lax.broadcasted_iota(I32, (768, 1), 0)
-    in_first = row < 384
-    low_row = jnp.where(in_first, row, row - 384)
-    nth = (low_row >= 96).astype(I32) + (low_row >= 192).astype(I32) + (low_row >= 288).astype(I32)
-    low_row = low_row - nth * 96
-    base = jnp.where(in_first, nth * 768 + low_row, nth * 192 + 96 + low_row)
-    lane = lax.broadcasted_iota(I32, (768, 256), 1)
+    for part in range(2):
+        for half in range(2):
+            spread(half, 1, part)
+
+    lane = lax.broadcasted_iota(I32, (1, 256), 1)
     query = lane // 16 * 32 + lane % 16
 
-    def turn_of(chunk):
-        return chunk + lax.div(chunk, 2) - 2 * lax.div(chunk, 3)
-
     def build(chunk):
-        turn = (0, 1, 3, 2)[chunk]
-        b, a = up(me.y, turn), up(me.x, turn)
-        kc[chunk, pl.ds(0, 384), pl.ds(0, 576)] = keys[:, b, pl.ds(0, 96), :].reshape(384, 576)
-        kc[chunk, pl.ds(384, 384), pl.ds(0, 576)] = keys[a, :, pl.ds(96, 96), :].reshape(384, 576)
+        for half in range(2):
+            mine = me.x if half else me.y
+            at = pl.ds(half * 384, 384)
+            rows = pl.ds(half * 96, 96)
+            if chunk in (0, 3):
+                n = up(mine, 0 if chunk == 0 else 2)
+                block = keys[n, :, rows, :] if half else keys[:, n, rows, :]
+                kc[chunk, at, pl.ds(0, 576)] = block.reshape(384, 576)
+                continue
+            two = pl.ds(chunk * 2 - 2, 2)
+            for k, n in enumerate((1, 3)):
+                n = up(mine, n)
+                block = keys[n, two, rows, :] if half else keys[two, n, rows, :]
+                kc[chunk, pl.ds(half * 384 + k * 192, 192), pl.ds(0, 576)] = block.reshape(192, 576)
         vt[chunk] = kc[chunk, :, pl.ds(0, 512)].T
+
+    low_row = lax.broadcasted_iota(I32, (96, 128), 0) - off_ref[0]
+    for chunk in range(4):
+        for half in range(2):
+            for k in range(4):
+                step, order = (0 if chunk == 0 else 2), k
+                if chunk in (1, 2):
+                    step, order = (1, 3)[k // 2], k % 2 + chunk * 2 - 2
+                across = up(me.x if half else me.y, step)
+                block = across * 4 + order if half else order * 4 + across
+                places[chunk, pl.ds((half * 4 + k) * 96, 96)] = low_row + (block * 192 + half * 96)
 
     def heads(tile):
         for g in range(2):
-            context = (acc[tile, g] / tot[tile, g]).astype(BF16)
+            context = (acc[tile, g] * (1.0 / tot[tile, g])).astype(BF16)
             for k in range(2):
                 value = dot(vupt[2 * g + k], context[:, k * 256 : k * 256 + 256]).T.astype(BF16)
                 ho[tile, :, :, :, pl.ds((2 * g + k) * 128, 128)] = value.reshape(4, 4, 16, 128)
@@ -549,14 +563,14 @@
         @pl.when(i == 1)
         def _():
             for half in range(2):
-                forward(half, 1)
+                forward(half, 1, 0)
             build(1)
-            build(2)
 
         @pl.when(i == 2)
         def _():
-            for half in range(2):
-                far(half, 1)
+            for part in range(2):
+                for half in range(2):
+                    far(half, 1, part)
             build(3)
             for k, n in enumerate((3, 1, 2)):
                 got = slabs.at[up(me.z, n), me.c]
@@ -573,7 +587,7 @@
             finish(0)
 
         tiles = (lax.div(i, 3), jnp.where(i == 1, 0, 1))
-        chunks = (turn_of(i), jnp.where(i == 1, 2, jnp.where(i == 2, 1, i)))
+        chunks = (i + lax.div(i, 2) - 2 * lax.div(i, 3), jnp.where(i == 1, 2, jnp.where(i == 2, 1, i)))
 
         def score(u):
             scores[u % 2] = dot(kc[chunks[u // 2]], qt[tiles[u // 2], u % 2])
@@ -590,10 +604,9 @@
             if u > 0:
                 gather_values(u - 1)
             if g == 0:
-                turn = turn_of(chunks[u // 2])
-                start = jnp.where(in_first, up(me.y, turn) * 192, up(me.x, turn) * 768)
-                limit = query + (tile * 16 + off_ref[0])
-                bias[...] = jnp.where(base + start <= limit, 0.0, LOWEST)
+                place = places[chunks[u // 2]]
+                place = jnp.concatenate([place, place], axis=1)
+                bias[...] = jnp.where(place <= query + tile * 16, 0.0, LOWEST)
             for k in range(2):
                 lanes = pl.ds(k * 256, 256)
                 s = scores[g, :, lanes] * scale + bias[...]
@@ -605,6 +618,14 @@
                 tot[tile, g, :, lanes] = tot[tile, g, :, lanes] * shrink + jnp.sum(p, axis=0, keepdims=True)
                 acc[tile, g, :, lanes] = acc[tile, g, :, lanes] * shrink
                 probs[g, :, lanes] = p.astype(BF16)
+            if u == 0:
+
+                @pl.when(i == 1)
+                def _():
+                    for half in range(2):
+                        forward(half, 1, 1)
+                    build(2)
+
             if u == 1:
 
                 @pl.when(i == 3)
@@ -615,12 +636,12 @@
         return carry
 
     lax.fori_loop(0, 4, step, 0)
+    finish(1)
     middle(0)
-    finish(1)
+    second(1, 0)
     second(0, 1)
-    second(1, 0)
+    middle(1)
     settle(0)
-    middle(1)
     second(1, 1)
     settle(1)
     for k, n in enumerate((3, 1, 2)):
@@ -628,10 +649,10 @@
         whole(slabs.at[up(me.z, n), me.c], w_s.at[4 + k])
     whole(mine, w_s.at[0])
     for half in range(2):
-        for phase in range(2):
+        for phase, part in ((0, 0), (1, 0), (1, 1)):
             for k in range(2):
-                whole(spot(half, phase, 0, 0, 96), k_s.at[sem(half, phase, k)])
-                whole(spot(half, phase, 0, 0, 48), k_s.at[sem(half, phase, 2 + k)])
+                whole(spot(half, phase, 0, 0, 96, part), k_s.at[sem(half, phase, k, part)])
+                whole(spot(half, phase, 0, 0, 48, part), k_s.at[sem(half, phase, 2 + k, part)])
     for tile in range(2):
         for h in range(2):
             for phase in range(2):
@@ -654,6 +675,7 @@
             pltpu.VMEM((4, 512, 768), BF16),
             pltpu.VMEM((2, 2, 640, 512), BF16),
             pltpu.VMEM((4, 128, 512), BF16),
+            pltpu.VMEM((4, 768, 128), I32),
             pltpu.VMEM((768, 256), F32),
             pltpu.VMEM((2, 768, 512), F32),
             pltpu.VMEM((2, 768, 512), BF16),
@@ -673,8 +695,8 @@
             pltpu.VMEM((2, 2, 16, 896), BF16),
             pltpu.VMEM((2, 2, 16, 1792), BF16),
             pltpu.VMEM((2, 2, 16, 1792), BF16),
-            dma((16,)),
-            dma((16,)),
+            dma((24,)),
+            dma((24,)),
             dma((7,)),
             dma((7,)),
             dma(()),

time: 161 us -> 158 us (0.981)
  Pallas kernels: 158 us -> 156 us
    pallas_call x1, Pallas kernels: 89.5 us -> 87.8 us  [back(): pl.pallas_call(back_kernel, out_shape=jax.ShapeDtypeStruct((32, 3584), F3...]
where the time goes in v6:
time: 158 us
  Pallas kernels  156 us (99%)
  other arithmetic  1.73 us (1%)
    pallas_call x1, Pallas kernels, back(): pl.pallas_call(back_kernel, out_shape=jax.ShapeDtypeStruct((32, 3584), F3...  87.8 us
    pallas_call x1, Pallas kernels, front(): pl.pallas_call(functools.partial(front_kernel, scale), out_shape=jax.Shap...  68.1 us

profile of v6, /device:TPU:1, one launch (start us, length us, event | category | flops | bytes accessed | tf_op | source)
XLA Modules:
  0.0 158.3 jit_solution(13054242042623003657)
XLA Ops:
  0.7 68.1 %front.1.stream_ref = f32[32,3584]{1,0:T(8,128)} custom-call(s32[1]{0:T(128)S(6)} %copy.12.off_ref, bf16[16,32,2304]{2,1,0:T(8,128)(2,1)} %bitcast.9, bf16[192,576]{1,0:T(8,128)(2,1)} %bitcast.11, bf16[4,512,128]{2,1,0:T(8,128)(2,1)} %vup_ref.1, bf16[448,512]{1,0:T(8,128)(2,1)} %bitcast.10, bf16[32,3584]{1,0:T(8,128)(2,1)} %resid_ref.1), custom_call_target="tpu_custom_call" | custom-call | tf_op jit(solution)/shard_map/front/pallas_call | solution.py:667
  68.7 87.8 %back.1 = f32[32,3584]{1,0:T(8,128)} custom-call(f32[32,3584]{1,0:T(8,128)} %front.1.stream_ref, f32[3584]{0:T(1024)} %gain_ref.1, s32[8,32]{1,0:T(8,128)} %bitcast.12, f32[8,32]{1,0:T(8,128)} %bitcast.13, bf16[3584,2048]{1,0:T(8,128)(2,1)} %bitcast.7, bf16[1024,3584]{1,0:T(8,128)(2,1)} %bitcast.8), custom_call_target="tpu_custom_call" | custom-call | tf_op jit(solution)/shard_map/back/pallas_call | solution.py:299
  156.6 1.7 %convert_element_type.3 = bf16[32,3584]{1,0:T(8,128)(2,1)} convert(f32[32,3584]{1,0:T(8,128)} %back.1) | non-fusion elementwise | flops 114688 | bytes 688128 | tf_op jit(solution)/shard_map/convert_element_type | solution.py:734

commit v7 on v6

--- a/solution.py
+++ b/solution.py
@@ -80,7 +80,7 @@
 def back_kernel(
     stream_ref, gain_ref, routes_ref, weights_ref, win_hbm, wdown_hbm,
     out_ref,
-    win, wdown, part4, turned, table_ref, metas, pick, wgt, swap,
+    win, wdown, part4, turned, table_ref, metas, ranks, pick, wgt, swap,
     nrm, toks, outg, rows, stage, hid, half_sum, psum, other_core, recv,
     wsem, m_s, m_r, g_s, g_r, d_s, d_r, t_s, t_r, x_s, x_r, c_s, c_r,
 ):
@@ -147,32 +147,40 @@
     spread = jnp.where(lane // 16 == lax.broadcasted_iota(I32, (128, 256), 0), 1.0, 0.0).astype(BF16)
     of_source = other % 16 // 2 == token // 32
     rank_wanted = (other % 2).astype(F32)
+    rx, ry, rz, low = token // 64, token // 16 % 4, token // 4 % 4, token % 4
+    swap[0] = jnp.where(other == rz * 64 + ry * 16 + rx * 4 + low, 1.0, 0.0).astype(BF16)
+    swap[1] = jnp.where(other == rx * 64 + rz * 16 + ry * 4 + low, 1.0, 0.0).astype(BF16)
+    column = lax.broadcasted_iota(I32, (256, 128), 1)
+
+    def wanted(part):
+        return jnp.where(column < 16, me.expert(part, column), -1).astype(F32)
+
+    def picks(part, half):
+        pick[part, half] = jnp.where(ranks[part] == half * 2.0, 1.0, 0.0).T.astype(BF16)
+
+    def weigh(part):
+        table, asked = metas[part].reshape(256, 128), wanted(part)
+        weight = jnp.zeros((256, 128), F32)
+        for k in range(8):
+            weight = jnp.where(table[:, k : k + 1] == asked, table[:, 8 + k : 9 + k], weight)
+        weight = dot(weight.astype(BF16), spread)
+        for half in range(2):
+            wgt[part, half] = jnp.where(ranks[part] == half * 2.0, weight, 0.0).astype(BF16)
+
     for part in range(3):
         whole(metas.at[part], m_r.at[part])
-        table = metas[part].reshape(256, 128)
-        column = lax.broadcasted_iota(I32, (256, 128), 1)
-        wanted = jnp.where(column < 16, me.expert(part, column), -1).astype(F32)
+        table, asked = metas[part].reshape(256, 128), wanted(part)
         hit = jnp.zeros((256, 128), F32)
-        weight = jnp.zeros((256, 128), F32)
         for k in range(8):
-            same = table[:, k : k + 1] == wanted
-            hit = jnp.where(same, 1.0, hit)
-            weight = jnp.where(same, table[:, 8 + k : 9 + k], weight)
+            hit = jnp.where(table[:, k : k + 1] == asked, 1.0, hit)
         rank = dot(earlier, hit.astype(BF16))
         rank = jnp.where(hit > 0.5, rank, -1.0)
-        rank = jnp.where(of_source, dot(rank.astype(BF16), spread) - rank_wanted, -1.0)
-        weight = dot(weight.astype(BF16), spread)
-        for half in range(2):
-            chosen = rank == half * 2.0
-            pick[part, half] = jnp.where(chosen, 1.0, 0.0).T.astype(BF16)
-            wgt[part, half] = jnp.where(chosen, weight, 0.0).astype(BF16)
+        ranks[part] = jnp.where(of_source, dot(rank.astype(BF16), spread) - rank_wanted, -1.0)
+        picks(part, 0)
         if part == 1:
             pass_on(0)
             pass_on(1)
     pass_on(2)
-    rx, ry, rz, low = token // 64, token // 16 % 4, token // 4 % 4, token % 4
-    swap[0] = jnp.where(other == rz * 64 + ry * 16 + rx * 4 + low, 1.0, 0.0).astype(BF16)
-    swap[1] = jnp.where(other == rx * 64 + rz * 16 + ry * 4 + low, 1.0, 0.0).astype(BF16)
 
     def half_of(ref, half):
         if ref is part4:
@@ -246,7 +254,11 @@
             exchange(half, outg, lambda part: part4, t_s, t_r, PARTS)
 
     dispatch(0)
+    for part in range(3):
+        picks(part, 1)
     dispatch(1)
+    for part in range(3):
+        weigh(part)
     expert(0)
     expert(1)
 
@@ -308,6 +320,7 @@
             pltpu.VMEM((128, 128), F32),
             pltpu.VMEM((32, 128), F32),
             pltpu.VMEM((3, 8, 32, 128), F32),
+            pltpu.VMEM((3, 256, 256), F32),
             pltpu.VMEM((3, 2, 256, 256), BF16),
             pltpu.VMEM((3, 2, 256, 256), BF16),
             pltpu.VMEM((2, 256, 256), BF16),

time: 158 us -> 159 us (level)
  no operation moved by 1% of the time
where the time goes in v7:
time: 159 us
  Pallas kernels  157 us (99%)
  other arithmetic  1.73 us (1%)
    pallas_call x1, Pallas kernels, back(): pl.pallas_call(back_kernel, out_shape=jax.ShapeDtypeStruct((32, 3584), F3...  88.5 us
    pallas_call x1, Pallas kernels, front(): pl.pallas_call(functools.partial(front_kernel, scale), out_shape=jax.Shap...  68.1 us

profile of v7, /device:TPU:1, one launch (start us, length us, event | category | flops | bytes accessed | tf_op | source)
XLA Modules:
  0.0 158.9 jit_solution(7962708831066472647)
XLA Ops:
  0.7 68.1 %front.1.stream_ref = f32[32,3584]{1,0:T(8,128)} custom-call(s32[1]{0:T(128)S(6)} %copy.12.off_ref, bf16[16,32,2304]{2,1,0:T(8,128)(2,1)} %bitcast.9, bf16[192,576]{1,0:T(8,128)(2,1)} %bitcast.11, bf16[4,512,128]{2,1,0:T(8,128)(2,1)} %vup_ref.1, bf16[448,512]{1,0:T(8,128)(2,1)} %bitcast.10, bf16[32,3584]{1,0:T(8,128)(2,1)} %resid_ref.1), custom_call_target="tpu_custom_call" | custom-call | tf_op jit(solution)/shard_map/front/pallas_call | solution.py:680
  68.7 88.5 %back.1 = f32[32,3584]{1,0:T(8,128)} custom-call(f32[32,3584]{1,0:T(8,128)} %front.1.stream_ref, f32[3584]{0:T(1024)} %gain_ref.1, s32[8,32]{1,0:T(8,128)} %bitcast.12, f32[8,32]{1,0:T(8,128)} %bitcast.13, bf16[3584,2048]{1,0:T(8,128)(2,1)} %bitcast.7, bf16[1024,3584]{1,0:T(8,128)(2,1)} %bitcast.8), custom_call_target="tpu_custom_call" | custom-call | tf_op jit(solution)/shard_map/back/pallas_call | solution.py:311
  157.2 1.7 %convert_element_type.3 = bf16[32,3584]{1,0:T(8,128)(2,1)} convert(f32[32,3584]{1,0:T(8,128)} %back.1) | non-fusion elementwise | flops 114688 | bytes 688128 | tf_op jit(solution)/shard_map/convert_element_type | solution.py:747

commit v8 on v7

--- a/solution.py
+++ b/solution.py
@@ -301,6 +301,21 @@
         whole(other_core.at[:, :, cols], x_s.at[part])
         whole(recv.at[pl.ds(0, 3), :, cols], c_s.at[part])
         whole(metas.at[part, pl.ds(0, 7)], m_s.at[part])
+
+
+def round_kernel(in_ref, out_ref):
+    out_ref[...] = in_ref[...].astype(BF16)
+
+
+def rounded(value):
+    vmem = pl.BlockSpec(memory_space=pltpu.VMEM)
+    return pl.pallas_call(
+        round_kernel,
+        out_shape=jax.ShapeDtypeStruct(value.shape, BF16),
+        in_specs=[vmem],
+        out_specs=vmem,
+        name="rounded",
+    )(value)
 
 
 def back(stream, norm_gain, routes, weights, expert_in, expert_down):
@@ -744,7 +759,7 @@
         score_scale * LOG2_E,
     )
     mixed = back(stream, norm_gain, routes.T, route_weights.T, expert_in[0], expert_down[0])
-    return mixed.astype(BF16)
+    return rounded(mixed)
 
 
 def solution(mesh):

time: 159 us -> 159 us (level)
  other arithmetic: 1.73 us -> 0 us
    convert_element_type x1 -> x0, other arithmetic: 1.73 us -> none  [shards(): return mixed.astype(BF16)]
    pallas_call x0 -> x1, Pallas kernels: none -> 1.73 us  [rounded(): pl.pallas_call(round_kernel, out_shape=jax.ShapeDtypeStruct(value.shape,...]
where the time goes in v8:
time: 159 us
  Pallas kernels  158 us (99%)
    pallas_call x1, Pallas kernels, back(): pl.pallas_call(back_kernel, out_shape=jax.ShapeDtypeStruct((32, 3584), F3...  88.5 us
    pallas_call x1, Pallas kernels, front(): pl.pallas_call(functools.partial(front_kernel, scale), out_shape=jax.Shap...  68.1 us

profile of v8, /device:TPU:1, one launch (start us, length us, event | category | flops | bytes accessed | tf_op | source)
XLA Modules:
  0.0 158.9 jit_solution(11568809484247400207)
XLA Ops:
  0.7 68.1 %front.1.stream_ref = f32[32,3584]{1,0:T(8,128)} custom-call(s32[1]{0:T(128)S(6)} %copy.12.off_ref, bf16[16,32,2304]{2,1,0:T(8,128)(2,1)} %bitcast.9, bf16[192,576]{1,0:T(8,128)(2,1)} %bitcast.11, bf16[4,512,128]{2,1,0:T(8,128)(2,1)} %vup_ref.1, bf16[448,512]{1,0:T(8,128)(2,1)} %bitcast.10, bf16[32,3584]{1,0:T(8,128)(2,1)} %resid_ref.1), custom_call_target="tpu_custom_call" | custom-call | tf_op jit(solution)/shard_map/front/pallas_call | solution.py:695
  68.7 88.5 %back.1.in_ref = f32[32,3584]{1,0:T(8,128)} custom-call(f32[32,3584]{1,0:T(8,128)} %front.1.stream_ref, f32[3584]{0:T(1024)} %gain_ref.1, s32[8,32]{1,0:T(8,128)} %bitcast.12, f32[8,32]{1,0:T(8,128)} %bitcast.13, bf16[3584,2048]{1,0:T(8,128)(2,1)} %bitcast.7, bf16[1024,3584]{1,0:T(8,128)(2,1)} %bitcast.8), custom_call_target="tpu_custom_call" | custom-call | tf_op jit(solution)/shard_map/back/pallas_call | solution.py:326
  157.2 1.7 %rounded.1 = bf16[32,3584]{1,0:T(8,128)(2,1)} custom-call(f32[32,3584]{1,0:T(8,128)} %back.1.in_ref), custom_call_target="tpu_custom_call" | custom-call | tf_op jit(solution)/shard_map/rounded/pallas_call | solution.py:312
